TPU v7x, 512 devices: a whole 4x8x8 slice. The times are simulated.
512 devices in a mesh: state: 64 (over y_hi, z, x), lat: 8 (over y_lo, core).
Axes of the slice: x: 4, y: 8 (y_hi: 2, y_lo: 4; y = y_hi * 4 + y_lo), z: 8, core: 2. Of those that a mesh axis runs over, the one named last changes fastest.
Arguments:
- spins: int32 [64, 8, 128], P('state', 'lat'), may hold values from -1 to 1, as said below
- embed_w: bfloat16 [64, 9], replicated, may hold values from -2 to 2
- block_w: bfloat16 [16, 1, 2, 64, 576], replicated, may hold values from -0.25 to 0.25
- readout: bfloat16 [16, 64], replicated, may hold values from -0.09375 to 0.09375
- amp_cot: float32 [16, 64], replicated, may hold values from -6 to 6
Outputs:
- log_amp: float32 [16, 64], replicated
- block_grad: float32 [1024, 1, 2, 576], P('state')
- embed_grad: float32 [64, 9], replicated
Inputs may be any that keep to these rules, and one draw needn't show every extreme that they name: `spins`: every entry is -1 or +1.
All inputs are finite; a program needn't handle non-finite values.
Results may differ from a plain program's by a relative error of at most 0.00083.
Values may be sent and summed in bfloat16 or wider, within the bound.
No kernel may reach another device: no remote copies, remote signals or barrier semaphores. Data moves between devices by JAX's collectives and lax.ppermute only.
A program may use at most 64 MiB of HBM per device.

v0:
```python
import math

import jax
import jax.numpy as jnp
from jax import lax
from jax.sharding import PartitionSpec as P


def extended(block, sides, width):
    for axis, dim in sides:
        count = lax.axis_size(axis)
        forward = [(i, i + 1) for i in range(count - 1)]
        forward.append((count - 1, 0))
        backward = [(target, source) for source, target in forward]
        low = lax.ppermute(
            lax.slice_in_dim(block, block.shape[dim] - width, None, axis=dim), axis, forward
        )
        high = lax.ppermute(lax.slice_in_dim(block, 0, width, axis=dim), axis, backward)
        block = jnp.concatenate([low, block, high], axis=dim)
    return block


def swapped(value, axis, bit):
    mask = 2**bit
    pairs = [(source, source ^ mask) for source in range(lax.axis_size(axis))]
    return lax.ppermute(value, axis, pairs)


def make_patches(padded):
    row_count = padded.shape[2] - 2
    col_count = padded.shape[3] - 2
    pieces = []
    for step_x in range(3):
        for step_y in range(3):
            pieces.append(padded[:, :, step_x : step_x + row_count, step_y : step_y + col_count])
    return jnp.concatenate(pieces, axis=1)


def conv_apply(weight, patches):
    return jnp.einsum("ok,nkxy->noxy", weight, patches, preferred_element_type=jnp.float32)


def flipped(weight):
    out_count = weight.shape[0]
    in_count = weight.shape[1] // 9
    return jnp.transpose(weight.reshape(out_count, 9, in_count)[:, ::-1, :], (2, 1, 0)).reshape(
        in_count, 9 * out_count
    )


def grad_from(inner_field, cot_patches):
    channel_count = inner_field.shape[1]
    joined = jnp.einsum(
        "nqxy,nkxy->kq", inner_field, cot_patches, preferred_element_type=jnp.float32
    )
    turned = joined.reshape(9, -1, channel_count)[::-1]
    return jnp.transpose(turned, (1, 0, 2)).reshape(turned.shape[1], 9 * channel_count)


def spin_contract(cotan, padded):
    row_count = cotan.shape[2]
    col_count = cotan.shape[3]
    offset_parts = []
    for step_x in range(3):
        for step_y in range(3):
            window = padded[:, 0, step_x : step_x + row_count, step_y : step_y + col_count].astype(
                jnp.float32
            )
            offset_parts.append(
                jnp.einsum("ncxy,nxy->c", cotan, window, precision=lax.Precision.HIGHEST)
            )
    return jnp.stack(offset_parts, axis=1)


def silu_slope(pre_act):
    sigmoid_value = jax.nn.sigmoid(pre_act)
    return sigmoid_value * (1.0 + pre_act * (1.0 - sigmoid_value))


def extend(source):
    padded = extended(source, (("lat", 2),), 1)
    return jnp.concatenate([padded[..., -1:], padded, padded[..., :1]], axis=3)


def stack_pair(payload, partner, upper_half):
    return jnp.where(
        upper_half, jnp.concatenate([partner, payload], 0), jnp.concatenate([payload, partner], 0)
    )


def split_pair(summed, upper_half):
    half_count = summed.shape[0] // 2
    lower_part = summed[:half_count]
    upper_part = summed[half_count:]
    return (
        jnp.where(upper_half, upper_part, lower_part),
        jnp.where(upper_half, lower_part, upper_part),
    )


def join_features(payload, state_index, low_bits, all_bits):
    for bit_index in range(low_bits, all_bits):
        partner = swapped(payload, "state", bit_index)
        payload = stack_pair(payload, partner, state_index >> bit_index & 1 == 1)
    return payload


def spread_cotangent(summed, state_index, low_bits, all_bits):
    for bit_index in reversed(range(low_bits, all_bits)):
        kept_part, sent_part = split_pair(summed, state_index >> bit_index & 1 == 1)
        summed = kept_part + swapped(sent_part, "state", bit_index)
    return summed


def spread_grads(summed, state_index, low_bits):
    for bit_index in reversed(range(low_bits)):
        kept_part, sent_part = split_pair(summed, state_index >> bit_index & 1 == 1)
        summed = kept_part + swapped(sent_part, "state", bit_index)
    return summed


def run_state(in_first, extend_fn, w_state, v_float, cot_vector, site_scale):
    stream = in_first[:, :, 1:-1, 1:-1].astype(jnp.float32)
    block_index = 0
    z_one = conv_apply(w_state[block_index, 0], make_patches(in_first))
    g_one = jax.nn.silu(z_one).astype(jnp.bfloat16)
    stream = stream + conv_apply(w_state[block_index, 1], make_patches(extend_fn(g_one)))
    saved_list = [(in_first[:, :, 1:-1, 1:-1], z_one, g_one)]
    part_row = (
        jnp.einsum("c,kcxy->k", v_float, jax.nn.silu(stream), precision=lax.Precision.HIGHEST)
        * site_scale
    )
    d_stream = (
        (cot_vector * site_scale)[:, None, None, None]
        * v_float[None, :, None, None]
        * silu_slope(stream)
    )
    grad_list = [None] * w_state.shape[0]
    for block_index in reversed(range(w_state.shape[0])):
        inner_field, z_one, g_one = saved_list[block_index]
        dz_two = d_stream.astype(jnp.bfloat16)
        cot_two = make_patches(extend_fn(dz_two))
        grad_two = grad_from(g_one, cot_two)
        dz_one = (conv_apply(flipped(w_state[block_index, 1]), cot_two) * silu_slope(z_one)).astype(
            jnp.bfloat16
        )
        cot_one = make_patches(extend_fn(dz_one))
        grad_one = grad_from(inner_field, cot_one)
        d_stream = d_stream + conv_apply(flipped(w_state[block_index, 0]), cot_one)
        grad_list[block_index] = jnp.stack([grad_one, grad_two])
    return (part_row, jnp.stack(grad_list), d_stream)


def local(spins, embed_w, block_w, readout, amp_cot):
    state_total = lax.axis_size("state")
    lat_count = lax.axis_size("lat")
    state_count = block_w.shape[0]
    group_count = state_total // state_count
    low_bits = group_count.bit_length() - 1
    all_bits = state_total.bit_length() - 1
    state_index = lax.axis_index("state")
    my_state = state_index // group_count
    my_group = state_index % group_count
    held_count = spins.shape[0]
    site_scale = 1.0 / math.sqrt(spins.shape[1] * lat_count * spins.shape[2])
    w_state = lax.dynamic_index_in_dim(block_w, my_state, 0, keepdims=False)
    v_float = lax.dynamic_index_in_dim(readout, my_state, 0, keepdims=False).astype(jnp.float32)
    cot_row = lax.dynamic_index_in_dim(amp_cot, my_state, 0, keepdims=False).reshape(
        state_count, group_count, held_count
    )
    group_pick = (jnp.arange(group_count) == my_group).astype(jnp.float32)
    group_cot = jnp.sum(cot_row * group_pick[None, :, None], axis=1).reshape(
        state_count * held_count
    )
    spin_field = spins.astype(jnp.bfloat16)[:, None]
    spin_pad = extend(spin_field)
    h_zero = conv_apply(embed_w, make_patches(spin_pad)).astype(jnp.bfloat16)
    h_pad = extend(h_zero)
    in_first = join_features(h_pad, state_index, low_bits, all_bits)
    group_row, grad_stack, d_stream = run_state(
        in_first, extend, w_state, v_float, group_cot, site_scale
    )
    own_cot_field = spread_cotangent(d_stream, state_index, low_bits, all_bits)
    contrib = spin_contract(own_cot_field, spin_pad)
    state_pick = (jnp.arange(state_count) == my_state).astype(jnp.float32)
    spread_row = (
        group_row.reshape(state_count, 1, held_count) * group_pick[None, :, None]
    ).reshape(-1)
    amp_part = state_pick[:, None] * spread_row[None, :]
    log_amp, embed_grad = lax.psum((amp_part, contrib), ("state", "lat"))
    by_channel = jnp.transpose(grad_stack, (2, 0, 1, 3))
    own_rows = spread_grads(by_channel, state_index, low_bits)
    block_grad = lax.psum(own_rows, "lat")
    return (log_amp, block_grad, embed_grad)


def solution(mesh):
    return jax.shard_map(
        local,
        mesh=mesh,
        in_specs=(P("state", "lat", None), P(), P(), P(), P()),
        out_specs=(P(), P("state", None, None, None), P()),
        check_vma=False,
    )
```

profile of v0, /device:TPU:1, one launch (start us, length us, event | category | flops | bytes accessed | tf_op | source)
XLA Modules:
  0.0 407.7 jit_solution(13275533866061689292)
XLA Ops:
  8.0 8.8 %collective-permute-start.1 = (bf16[1,1,1,128]{3,2,1,0:T(2,128)(2,1)S(1)}, bf16[1,1,1,128]{3,2,1,0:T(2,128)(2,1)S(1)}, u32[]{:S(2)}, u32[]{:S(2)}) collective-permute-start(bf16[1,1,1,128]{3,2,1,0:T(2,128)(2,1)S(1)} %convert_bitcast_fusion), channel_id=1, source_target_pairs={{1,0},{2,1},{3,2},{4,3},{5,4},{6,5},{7,6},{0,7},{9,8},{10,9},{11,1... | collective-permute-start | bytes 776 | tf_op jit(solution)/shard_map/ppermute | solution.py:18
  16.8 1.9 collective-permute-start
  25.2 5.6 %collective-permute-start.3 = (bf16[1,64,1,128]{3,1,2,0:T(8,128)(2,1)S(1)}, bf16[1,64,1,128]{3,1,2,0:T(8,128)(2,1)S(1)}, u32[]{:S(2)}, u32[]{:S(2)}) collective-permute-start(bf16[1,64,1,128]{3,1,2,0:T(8,128)(2,1)S(1)} %fusion.29), channel_id=1, source_target_pairs={{1,0},{2,1},{3,2},{4,3},{5,4},{6,5},{7,6},{0,7},{9,8},{10,9},{11,1... | collective-permute-start | bytes 49160 | tf_op jit(solution)/shard_map/ppermute | solution.py:18
  30.8 1.9 collective-permute-start.2
  32.8 1.1 collective-permute-done.2
  34.1 1.9 collective-permute-start.4
  36.0 3.4 collective-permute-done.4
  39.6 4.1 %collective-permute-start.5 = (bf16[2,64,3,130]{3,1,2,0:T(8,128)(2,1)S(1)}, bf16[2,64,3,130]{3,1,2,0:T(8,128)(2,1)S(1)}, u32[]{:S(2)}, u32[]{:S(2)}) collective-permute-start(bf16[2,64,3,130]{3,1,2,0:T(8,128)(2,1)S(1)} %maximum_select_fusion.3), channel_id=1, source_target_pairs={{0,64},{8,72},{16,80},{24,88},{32,96},{40,104},{48,112},{56,120},{... | collective-permute-start | bytes 299528 | tf_op jit(solution)/shard_map/ppermute | solution.py:26
  44.5 4.5 %collective-permute-done.5 = bf16[2,64,3,130]{3,1,2,0:T(8,128)(2,1)S(1)} collective-permute-done((bf16[2,64,3,130]{3,1,2,0:T(8,128)(2,1)S(1)}, bf16[2,64,3,130]{3,1,2,0:T(8,128)(2,1)S(1)}, u32[]{:S(2)}, u32[]{:S(2)}) %collective-permute-start.5) | collective-permute-done | bytes 99872 | tf_op jit(solution)/shard_map/ppermute | solution.py:26
  49.2 8.3 %collective-permute-start.6 = (bf16[4,64,3,130]{3,1,2,0:T(8,128)(2,1)S(1)}, bf16[4,64,3,130]{3,1,2,0:T(8,128)(2,1)S(1)}, u32[]{:S(2)}, u32[]{:S(2)}) collective-permute-start(bf16[4,64,3,130]{3,1,2,0:T(8,128)(2,1)S(1)} %maximum_select_fusion.2), channel_id=1, source_target_pairs={{0,128},{8,136},{16,144},{24,152},{32,160},{40,168},{48,176},{56,1... | collective-permute-start | bytes 599048 | tf_op jit(solution)/shard_map/ppermute | solution.py:26
  58.0 7.0 %collective-permute-done.6 = bf16[4,64,3,130]{3,1,2,0:T(8,128)(2,1)S(1)} collective-permute-done((bf16[4,64,3,130]{3,1,2,0:T(8,128)(2,1)S(1)}, bf16[4,64,3,130]{3,1,2,0:T(8,128)(2,1)S(1)}, u32[]{:S(2)}, u32[]{:S(2)}) %collective-permute-start.6) | collective-permute-done | bytes 199712 | tf_op jit(solution)/shard_map/ppermute | solution.py:26
  65.3 4.8 %collective-permute-start.7 = (bf16[8,64,3,130]{3,1,2,0:T(8,128)(2,1)S(1)}, bf16[8,64,3,130]{3,1,2,0:T(8,128)(2,1)}, u32[]{:S(2)}, u32[]{:S(2)}) collective-permute-start(bf16[8,64,3,130]{3,1,2,0:T(8,128)(2,1)S(1)} %maximum_select_fusion.1), channel_id=1, source_target_pairs={{0,256},{8,264},{16,272},{24,280},{32,288},{40,296},{48,304},{56,3... | collective-permute-start | bytes 1198088 | tf_op jit(solution)/shard_map/ppermute | solution.py:26
  71.3 11.7 %collective-permute-done.7 = bf16[8,64,3,130]{3,1,2,0:T(8,128)(2,1)} collective-permute-done((bf16[8,64,3,130]{3,1,2,0:T(8,128)(2,1)S(1)}, bf16[8,64,3,130]{3,1,2,0:T(8,128)(2,1)}, u32[]{:S(2)}, u32[]{:S(2)}) %collective-permute-start.7) | collective-permute-done | bytes 399392 | tf_op jit(solution)/shard_map/ppermute | solution.py:26
  83.0 1.9 maximum_select_fusion
  86.5 1.4 multiply_convert_fusion
  87.9 10.2 %collective-permute-start.9 = (bf16[16,64,1,128]{3,1,2,0:T(8,128)(2,1)S(1)}, bf16[16,64,1,128]{3,1,2,0:T(8,128)(2,1)S(1)}, u32[]{:S(2)}, u32[]{:S(2)}) collective-permute-start(bf16[16,64,1,128]{3,1,2,0:T(8,128)(2,1)S(1)} %get-tuple-element.37), channel_id=1, source_target_pairs={{1,0},{2,1},{3,2},{4,3},{5,4},{6,5},{7,6},{0,7},{9,8},{10,9},{11,1... | collective-permute-start | bytes 786440 | tf_op jit(solution)/shard_map/ppermute | solution.py:18
  98.1 23.5 %collective-permute-start.8 = (bf16[16,64,1,128]{3,1,2,0:T(8,128)(2,1)S(1)}, bf16[16,64,1,128]{3,1,2,0:T(8,128)(2,1)S(1)}, u32[]{:S(2)}, u32[]{:S(2)}) collective-permute-start(bf16[16,64,1,128]{3,1,2,0:T(8,128)(2,1)S(1)} %get-tuple-element.37), channel_id=1, source_target_pairs={{0,1},{1,2},{2,3},{3,4},{4,5},{5,6},{6,7},{7,0},{8,9},{9,10},{10,1... | collective-permute-start | bytes 786440 | tf_op jit(solution)/shard_map/ppermute | solution.py:15
  121.6 1.2 bitcast_convert_fusion
  127.8 3.1 fusion.67
  130.9 5.1 %collective-permute-start.11 = (bf16[16,64,1,128]{3,1,2,0:T(8,128)(2,1)S(1)}, bf16[16,64,1,128]{3,1,2,0:T(8,128)(2,1)S(1)}, u32[]{:S(2)}, u32[]{:S(2)}) collective-permute-start(bf16[16,64,1,128]{3,1,2,0:T(8,128)(2,1)S(1)} %get-tuple-element.23), channel_id=1, source_target_pairs={{1,0},{2,1},{3,2},{4,3},{5,4},{6,5},{7,6},{0,7},{9,8},{10,9},{11,1... | collective-permute-start | bytes 786440 | tf_op jit(solution)/shard_map/ppermute | solution.py:18
  136.0 1.9 collective-permute-start.10
  139.8 1.7 copy.24
  143.2 1.7 copy.33
  148.9 1.2 maximum_dynamic-update-slice_fusion.6
  152.5 2.4 collective-permute-start.13
  154.9 3.3 collective-permute-start.12
  159.7 1.8 copy.27
  161.6 2.5 collective-permute-done.12
  167.6 1.2 maximum_dynamic-update-slice_fusion.2
  170.0 2.3 convolution_bitcast_fusion.1
  174.5 4.6 %collective-permute-start.14 = (f32[32,1,2,576]{3,0,2,1:T(8,128)}, f32[32,1,2,576]{3,0,2,1:T(8,128)S(1)}, u32[]{:S(2)}, u32[]{:S(2)}) collective-permute-start(f32[32,1,2,576]{3,0,2,1:T(8,128)} %copy.28), channel_id=1, source_target_pairs={{0,16},{8,24},{16,0},{24,8},{32,48},{40,56},{48,32},{56,40},{64,80... | collective-permute-start | bytes 442376 | tf_op jit(solution)/shard_map/ppermute | solution.py:26
  179.2 2.6 fusion.20
  182.5 7.1 %collective-permute-start.16 = (f32[8,64,1,128]{3,1,2,0:T(8,128)S(1)}, f32[8,64,1,128]{3,1,2,0:T(8,128)}, u32[]{:S(2)}, u32[]{:S(2)}) collective-permute-start(f32[8,64,1,128]{3,1,2,0:T(8,128)S(1)} %slice_select_fusion.2), channel_id=1, source_target_pairs={{0,256},{8,264},{16,272},{24,280},{32,288},{40,296},{48,304},{56,3... | collective-permute-start | bytes 786440 | tf_op jit(solution)/shard_map/ppermute | solution.py:26
  190.7 1.7 select_add_fusion.1
  193.4 1.3 copy.30
  194.7 2.2 collective-permute-start.15
  196.9 4.2 %collective-permute-done.16 = f32[8,64,1,128]{3,1,2,0:T(8,128)} collective-permute-done((f32[8,64,1,128]{3,1,2,0:T(8,128)S(1)}, f32[8,64,1,128]{3,1,2,0:T(8,128)}, u32[]{:S(2)}, u32[]{:S(2)}) %collective-permute-start.16) | collective-permute-done | bytes 262176 | tf_op jit(solution)/shard_map/ppermute | solution.py:26
  201.1 1.1 select_add_fusion.2
  202.9 6.2 %collective-permute-start.17 = (f32[4,64,1,128]{3,1,2,0:T(8,128)}, f32[4,64,1,128]{3,1,2,0:T(8,128)}, u32[]{:S(2)}, u32[]{:S(2)}) collective-permute-start(f32[4,64,1,128]{3,1,2,0:T(8,128)} %slice_select_fusion.3), channel_id=1, source_target_pairs={{0,128},{8,136},{16,144},{24,152},{32,160},{40,168},{48,176},{56,1... | collective-permute-start | bytes 393224 | tf_op jit(solution)/shard_map/ppermute | solution.py:26
  210.7 1.3 mul.119
  212.0 1.2 mul.122
  213.2 1.9 copy.31
  216.8 5.6 %collective-permute-start.18 = (f32[2,64,1,128]{3,1,2,0:T(8,128)S(1)}, f32[2,64,1,128]{3,1,2,0:T(8,128)S(1)}, u32[]{:S(2)}, u32[]{:S(2)}) collective-permute-start(f32[2,64,1,128]{3,1,2,0:T(8,128)S(1)} %slice_select_fusion.4), channel_id=1, source_target_pairs={{0,64},{8,72},{16,80},{24,88},{32,96},{40,104},{48,112},{56,120},{... | collective-permute-start | bytes 196616 | tf_op jit(solution)/shard_map/ppermute | solution.py:26
  222.4 2.1 select_add_fusion
  224.6 1.9 collective-permute-start.19
  226.6 69.0 %all-reduce.3.cloned.1.call-done = f32[16,1,2,576]{0,3,2,1:T(8,128)} async-done(((f32[16,1,2,576]{0,3,2,1:T(8,128)}), f32[16,1,2,576]{0,3,2,1:T(8,128)}) %all-reduce.3.cloned.1.call-update) | async-done | bytes 73744 | tf_op jit(solution)/shard_map/psum | solution.py:193
  295.7 1.9 copy.35
  299.1 101.8 %all-reduce = (f32[16,64]{1,0:T(8,128)}, f32[64,9]{0,1:T(8,128)}) all-reduce(f32[16,64]{1,0:T(8,128)S(1)} %broadcast_multiply_fusion.1, f32[64,9]{0,1:T(8,128)S(1)} %stack.47), channel_id=1, replica_groups=mesh['state'=64,'lat'=8] {'state','lat'}, use_global_device_ids=true, to_apply=%region_1.2 | all-reduce | flops 1600 | bytes 12800 | tf_op jit(solution)/shard_map/psum | solution.py:190
  (177 shorter events, 43.4 us)
Async XLA Ops:
  7.2 63.4 %copy-start = (bf16[16,1,2,64,576]{4,3,2,1,0:T(8,128)(2,1)S(1)}, bf16[16,1,2,64,576]{4,3,2,1,0:T(8,128)(2,1)}, u32[]{:S(2)}) copy-start(bf16[16,1,2,64,576]{4,3,2,1,0:T(8,128)(2,1)} %param.7) | copy-start | bytes 7077892
  7.2 288.5 %all-reduce.3.cloned.1.call-start = ((), (), s32[]{:S(2)}) async-start(), calls=%async_computation | async-start | bytes 1179648 | tf_op jit(solution)/shard_map/psum | solution.py:193
  8.0 10.7 %collective-permute-start.1 = (bf16[1,1,1,128]{3,2,1,0:T(2,128)(2,1)S(1)}, bf16[1,1,1,128]{3,2,1,0:T(2,128)(2,1)S(1)}, u32[]{:S(2)}, u32[]{:S(2)}) collective-permute-start(bf16[1,1,1,128]{3,2,1,0:T(2,128)(2,1)S(1)} %convert_bitcast_fusion), channel_id=1, source_target_pairs={{1,0},{2,1},{3,2},{4,3},{5,4},{6,5},{7,6},{0,7},{9,8},{10,9},{11,1... | collective-permute-start | bytes 776 | tf_op jit(solution)/shard_map/ppermute | solution.py:18
  16.8 3.0 collective-permute-start
  18.8 14.0 %copy-start.11 = (bf16[1,1,1,128]{3,2,1,0:T(2,128)(2,1)}, bf16[1,1,1,128]{3,2,1,0:T(2,128)(2,1)S(1)}, u32[]{:S(2)}) copy-start(bf16[1,1,1,128]{3,2,1,0:T(2,128)(2,1)S(1)} %collective-permute-done.1) | copy-start | bytes 772
  19.8 12.9 %copy-start.13 = (bf16[1,1,1,128]{3,2,1,0:T(2,128)(2,1)}, bf16[1,1,1,128]{3,2,1,0:T(2,128)(2,1)S(1)}, u32[]{:S(2)}) copy-start(bf16[1,1,1,128]{3,2,1,0:T(2,128)(2,1)S(1)} %collective-permute-done) | copy-start | bytes 772
  25.2 7.5 %collective-permute-start.3 = (bf16[1,64,1,128]{3,1,2,0:T(8,128)(2,1)S(1)}, bf16[1,64,1,128]{3,1,2,0:T(8,128)(2,1)S(1)}, u32[]{:S(2)}, u32[]{:S(2)}) collective-permute-start(bf16[1,64,1,128]{3,1,2,0:T(8,128)(2,1)S(1)} %fusion.29), channel_id=1, source_target_pairs={{1,0},{2,1},{3,2},{4,3},{5,4},{6,5},{7,6},{0,7},{9,8},{10,9},{11,1... | collective-permute-start | bytes 49160 | tf_op jit(solution)/shard_map/ppermute | solution.py:18
  30.8 3.1 collective-permute-start.2
  34.1 5.4 %collective-permute-start.4 = (bf16[1,64,3,130]{3,1,2,0:T(8,128)(2,1)S(1)}, bf16[1,64,3,130]{3,1,2,0:T(8,128)(2,1)S(1)}, u32[]{:S(2)}, u32[]{:S(2)}) collective-permute-start(bf16[1,64,3,130]{3,1,2,0:T(8,128)(2,1)S(1)} %pad_maximum_fusion.21), channel_id=1, source_target_pairs={{0,32},{8,40},{16,48},{24,56},{32,0},{40,8},{48,16},{56,24},{64,96... | collective-permute-start | bytes 149768 | tf_op jit(solution)/shard_map/ppermute | solution.py:26
  39.6 9.4 %collective-permute-start.5 = (bf16[2,64,3,130]{3,1,2,0:T(8,128)(2,1)S(1)}, bf16[2,64,3,130]{3,1,2,0:T(8,128)(2,1)S(1)}, u32[]{:S(2)}, u32[]{:S(2)}) collective-permute-start(bf16[2,64,3,130]{3,1,2,0:T(8,128)(2,1)S(1)} %maximum_select_fusion.3), channel_id=1, source_target_pairs={{0,64},{8,72},{16,80},{24,88},{32,96},{40,104},{48,112},{56,120},{... | collective-permute-start | bytes 299528 | tf_op jit(solution)/shard_map/ppermute | solution.py:26
  49.2 15.8 %collective-permute-start.6 = (bf16[4,64,3,130]{3,1,2,0:T(8,128)(2,1)S(1)}, bf16[4,64,3,130]{3,1,2,0:T(8,128)(2,1)S(1)}, u32[]{:S(2)}, u32[]{:S(2)}) collective-permute-start(bf16[4,64,3,130]{3,1,2,0:T(8,128)(2,1)S(1)} %maximum_select_fusion.2), channel_id=1, source_target_pairs={{0,128},{8,136},{16,144},{24,152},{32,160},{40,168},{48,176},{56,1... | collective-permute-start | bytes 599048 | tf_op jit(solution)/shard_map/ppermute | solution.py:26
  65.3 17.7 %collective-permute-start.7 = (bf16[8,64,3,130]{3,1,2,0:T(8,128)(2,1)S(1)}, bf16[8,64,3,130]{3,1,2,0:T(8,128)(2,1)}, u32[]{:S(2)}, u32[]{:S(2)}) collective-permute-start(bf16[8,64,3,130]{3,1,2,0:T(8,128)(2,1)S(1)} %maximum_select_fusion.1), channel_id=1, source_target_pairs={{0,256},{8,264},{16,272},{24,280},{32,288},{40,296},{48,304},{56,3... | collective-permute-start | bytes 1198088 | tf_op jit(solution)/shard_map/ppermute | solution.py:26
  70.6 15.9 %copy-start.7 = (bf16[1,2,64,576]{3,2,1,0:T(8,128)(2,1)}, bf16[1,2,64,576]{3,2,1,0:T(8,128)(2,1)S(1)}, u32[]{:S(2)}) copy-start(bf16[1,2,64,576]{3,2,1,0:T(8,128)(2,1)S(1)} %dynamic-slice_bitcast_fusion) | copy-start | bytes 442372
  84.9 1.5 copy-start.2
  87.9 36.7 %collective-permute-start.9 = (bf16[16,64,1,128]{3,1,2,0:T(8,128)(2,1)S(1)}, bf16[16,64,1,128]{3,1,2,0:T(8,128)(2,1)S(1)}, u32[]{:S(2)}, u32[]{:S(2)}) collective-permute-start(bf16[16,64,1,128]{3,1,2,0:T(8,128)(2,1)S(1)} %get-tuple-element.37), channel_id=1, source_target_pairs={{1,0},{2,1},{3,2},{4,3},{5,4},{6,5},{7,6},{0,7},{9,8},{10,9},{11,1... | collective-permute-start | bytes 786440 | tf_op jit(solution)/shard_map/ppermute | solution.py:18
  98.1 27.3 %collective-permute-start.8 = (bf16[16,64,1,128]{3,1,2,0:T(8,128)(2,1)S(1)}, bf16[16,64,1,128]{3,1,2,0:T(8,128)(2,1)S(1)}, u32[]{:S(2)}, u32[]{:S(2)}) collective-permute-start(bf16[16,64,1,128]{3,1,2,0:T(8,128)(2,1)S(1)} %get-tuple-element.37), channel_id=1, source_target_pairs={{0,1},{1,2},{2,3},{3,4},{4,5},{5,6},{6,7},{7,0},{8,9},{9,10},{10,1... | collective-permute-start | bytes 786440 | tf_op jit(solution)/shard_map/ppermute | solution.py:15
  124.6 2.8 copy-start.16
  126.9 0.9 copy-start.8
  130.9 14.5 %collective-permute-start.11 = (bf16[16,64,1,128]{3,1,2,0:T(8,128)(2,1)S(1)}, bf16[16,64,1,128]{3,1,2,0:T(8,128)(2,1)S(1)}, u32[]{:S(2)}, u32[]{:S(2)}) collective-permute-start(bf16[16,64,1,128]{3,1,2,0:T(8,128)(2,1)S(1)} %get-tuple-element.23), channel_id=1, source_target_pairs={{1,0},{2,1},{3,2},{4,3},{5,4},{6,5},{7,6},{0,7},{9,8},{10,9},{11,1... | collective-permute-start | bytes 786440 | tf_op jit(solution)/shard_map/ppermute | solution.py:18
  136.0 9.4 %collective-permute-start.10 = (bf16[16,64,1,128]{3,1,2,0:T(8,128)(2,1)S(1)}, bf16[16,64,1,128]{3,1,2,0:T(8,128)(2,1)}, u32[]{:S(2)}, u32[]{:S(2)}) collective-permute-start(bf16[16,64,1,128]{3,1,2,0:T(8,128)(2,1)S(1)} %get-tuple-element.23), channel_id=1, source_target_pairs={{0,1},{1,2},{2,3},{3,4},{4,5},{5,6},{6,7},{7,0},{8,9},{9,10},{10,1... | collective-permute-start | bytes 786440 | tf_op jit(solution)/shard_map/ppermute | solution.py:15
  150.7 0.9 copy-start.10
  150.7 1.1 copy-start.28
  152.5 9.1 %collective-permute-start.13 = (bf16[16,64,1,128]{3,1,2,0:T(8,128)(2,1)S(1)}, bf16[16,64,1,128]{3,1,2,0:T(8,128)(2,1)S(1)}, u32[]{:S(2)}, u32[]{:S(2)}) collective-permute-start(bf16[16,64,1,128]{3,1,2,0:T(8,128)(2,1)S(1)} %fusion.26), channel_id=1, source_target_pairs={{1,0},{2,1},{3,2},{4,3},{5,4},{6,5},{7,6},{0,7},{9,8},{10,9},{11,1... | collective-permute-start | bytes 786440 | tf_op jit(solution)/shard_map/ppermute | solution.py:18
  154.9 9.2 %collective-permute-start.12 = (bf16[16,64,1,128]{3,1,2,0:T(8,128)(2,1)S(1)}, bf16[16,64,1,128]{3,1,2,0:T(8,128)(2,1)}, u32[]{:S(2)}, u32[]{:S(2)}) collective-permute-start(bf16[16,64,1,128]{3,1,2,0:T(8,128)(2,1)S(1)} %fusion.26), channel_id=1, source_target_pairs={{0,1},{1,2},{2,3},{3,4},{4,5},{5,6},{6,7},{7,0},{8,9},{9,10},{10,1... | collective-permute-start | bytes 786440 | tf_op jit(solution)/shard_map/ppermute | solution.py:15
  170.0 2.3 copy-start.15
  170.0 2.5 copy-start.6
  172.3 6.8 %copy-start.17 = (f32[16,64]{1,0:T(8,128)S(1)}, f32[16,64]{1,0:T(8,128)}, u32[]{:S(2)}) copy-start(f32[16,64]{1,0:T(8,128)} %copy-done.16) | copy-start | bytes 12292
  172.6 0.8 copy-start.1
  173.4 5.8 %copy-start.9 = (bf16[64,9,64]{0,2,1:T(8,128)(2,1)S(1)}, bf16[64,9,64]{0,2,1:T(8,128)(2,1)}, u32[]{:S(2)}) copy-start(bf16[64,9,64]{0,2,1:T(8,128)(2,1)} %copy.33) | copy-start | bytes 221188
  174.5 15.2 %collective-permute-start.14 = (f32[32,1,2,576]{3,0,2,1:T(8,128)}, f32[32,1,2,576]{3,0,2,1:T(8,128)S(1)}, u32[]{:S(2)}, u32[]{:S(2)}) collective-permute-start(f32[32,1,2,576]{3,0,2,1:T(8,128)} %copy.28), channel_id=1, source_target_pairs={{0,16},{8,24},{16,0},{24,8},{32,48},{40,56},{48,32},{56,40},{64,80... | collective-permute-start | bytes 442376 | tf_op jit(solution)/shard_map/ppermute | solution.py:26
  181.7 0.8 copy-start.3
  182.5 18.6 %collective-permute-start.16 = (f32[8,64,1,128]{3,1,2,0:T(8,128)S(1)}, f32[8,64,1,128]{3,1,2,0:T(8,128)}, u32[]{:S(2)}, u32[]{:S(2)}) collective-permute-start(f32[8,64,1,128]{3,1,2,0:T(8,128)S(1)} %slice_select_fusion.2), channel_id=1, source_target_pairs={{0,256},{8,264},{16,272},{24,280},{32,288},{40,296},{48,304},{56,3... | collective-permute-start | bytes 786440 | tf_op jit(solution)/shard_map/ppermute | solution.py:26
  194.7 18.5 %collective-permute-start.15 = (f32[16,1,2,576]{3,0,2,1:T(8,128)S(1)}, f32[16,1,2,576]{3,0,2,1:T(8,128)}, u32[]{:S(2)}, u32[]{:S(2)}) collective-permute-start(f32[16,1,2,576]{3,0,2,1:T(8,128)S(1)} %copy.30), channel_id=1, source_target_pairs={{0,8},{8,0},{16,24},{24,16},{32,40},{40,32},{48,56},{56,48},{64,72... | collective-permute-start | bytes 221192 | tf_op jit(solution)/shard_map/ppermute | solution.py:26
  202.9 12.2 %collective-permute-start.17 = (f32[4,64,1,128]{3,1,2,0:T(8,128)}, f32[4,64,1,128]{3,1,2,0:T(8,128)}, u32[]{:S(2)}, u32[]{:S(2)}) collective-permute-start(f32[4,64,1,128]{3,1,2,0:T(8,128)} %slice_select_fusion.3), channel_id=1, source_target_pairs={{0,128},{8,136},{16,144},{24,152},{32,160},{40,168},{48,176},{56,1... | collective-permute-start | bytes 393224 | tf_op jit(solution)/shard_map/ppermute | solution.py:26
  213.2 13.4 %copy-start.26 = (f32[16]{0:T(128)S(1)}, f32[16]{0:T(128)}, u32[]{:S(2)}) copy-start(f32[16]{0:T(128)} %compare_convert_fusion.1) | copy-start | bytes 196
  213.2 13.4 %copy-start.27 = (f32[64]{0:T(128)S(1)}, f32[64]{0:T(128)}, u32[]{:S(2)}) copy-start(f32[64]{0:T(128)} %mul.122) | copy-start | bytes 772
  215.2 82.4 %copy-start.25 = (s32[1,1,128]{2,1,0:T(1,128)S(1)}, s32[1,1,128]{2,1,0:T(1,128)}, u32[]{:S(2)}) copy-start(s32[1,1,128]{2,1,0:T(1,128)} %param.5) | copy-start | bytes 1540
  215.2 82.5 %copy-start.19 = (bf16[1,1,1,128]{3,2,1,0:T(2,128)(2,1)S(1)}, bf16[1,1,1,128]{3,2,1,0:T(2,128)(2,1)}, u32[]{:S(2)}) copy-start(bf16[1,1,1,128]{3,2,1,0:T(2,128)(2,1)} %get-tuple-element.20) | copy-start | bytes 772
  215.2 82.7 %copy-start.20 = (bf16[1,1,1,128]{3,2,1,0:T(2,128)(2,1)S(1)}, bf16[1,1,1,128]{3,2,1,0:T(2,128)(2,1)}, u32[]{:S(2)}) copy-start(bf16[1,1,1,128]{3,2,1,0:T(2,128)(2,1)} %get-tuple-element.18) | copy-start | bytes 772
  215.2 82.9 %copy-start.21 = (bf16[1,1,1,128]{3,2,1,0:T(2,128)(2,1)S(1)}, bf16[1,1,1,128]{3,2,1,0:T(2,128)(2,1)}, u32[]{:S(2)}) copy-start(bf16[1,1,1,128]{3,2,1,0:T(2,128)(2,1)} %get-tuple-element.16) | copy-start | bytes 772
  216.8 81.4 %copy-start.22 = (bf16[1,1,1,128]{3,2,1,0:T(2,128)(2,1)S(1)}, bf16[1,1,1,128]{3,2,1,0:T(2,128)(2,1)}, u32[]{:S(2)}) copy-start(bf16[1,1,1,128]{3,2,1,0:T(2,128)(2,1)} %get-tuple-element.14) | copy-start | bytes 772
  216.8 81.6 %copy-start.23 = (bf16[1,1,1,128]{3,2,1,0:T(2,128)(2,1)S(1)}, bf16[1,1,1,128]{3,2,1,0:T(2,128)(2,1)}, u32[]{:S(2)}) copy-start(bf16[1,1,1,128]{3,2,1,0:T(2,128)(2,1)} %get-tuple-element.12) | copy-start | bytes 772
  216.8 81.7 %copy-start.18 = (bf16[1,1,1,128]{3,2,1,0:T(2,128)(2,1)S(1)}, bf16[1,1,1,128]{3,2,1,0:T(2,128)(2,1)}, u32[]{:S(2)}) copy-start(bf16[1,1,1,128]{3,2,1,0:T(2,128)(2,1)} %get-tuple-element.22) | copy-start | bytes 772
  216.8 81.9 %copy-start.14 = (bf16[1,1,1,128]{3,2,1,0:T(2,128)(2,1)S(1)}, bf16[1,1,1,128]{3,2,1,0:T(2,128)(2,1)}, u32[]{:S(2)}) copy-start(bf16[1,1,1,128]{3,2,1,0:T(2,128)(2,1)} %copy-done.13) | copy-start | bytes 772
  216.8 82.0 %copy-start.12 = (bf16[1,1,1,128]{3,2,1,0:T(2,128)(2,1)S(1)}, bf16[1,1,1,128]{3,2,1,0:T(2,128)(2,1)}, u32[]{:S(2)}) copy-start(bf16[1,1,1,128]{3,2,1,0:T(2,128)(2,1)} %copy-done.11) | copy-start | bytes 772
  216.8 7.8 %copy-start.5 = (f32[4,64,1,128]{3,1,2,0:T(8,128)S(1)}, f32[4,64,1,128]{3,1,2,0:T(8,128)}, u32[]{:S(2)}) copy-start(f32[4,64,1,128]{3,1,2,0:T(8,128)} %copy-done.4) | copy-start | bytes 393220
  216.8 7.7 %collective-permute-start.18 = (f32[2,64,1,128]{3,1,2,0:T(8,128)S(1)}, f32[2,64,1,128]{3,1,2,0:T(8,128)S(1)}, u32[]{:S(2)}, u32[]{:S(2)}) collective-permute-start(f32[2,64,1,128]{3,1,2,0:T(8,128)S(1)} %slice_select_fusion.4), channel_id=1, source_target_pairs={{0,64},{8,72},{16,80},{24,88},{32,96},{40,104},{48,112},{56,120},{... | collective-permute-start | bytes 196616 | tf_op jit(solution)/shard_map/ppermute | solution.py:26
  224.6 72.9 %collective-permute-start.19 = (f32[1,64,1,128]{3,1,2,0:T(8,128)S(1)}, f32[1,64,1,128]{3,1,2,0:T(8,128)S(1)}, u32[]{:S(2)}, u32[]{:S(2)}) collective-permute-start(f32[1,64,1,128]{3,1,2,0:T(8,128)S(1)} %slice_select_fusion.5), channel_id=1, source_target_pairs={{0,32},{8,40},{16,48},{24,56},{32,0},{40,8},{48,16},{56,24},{64,96... | collective-permute-start | bytes 98312 | tf_op jit(solution)/shard_map/ppermute | solution.py:26
  (2 other events, 1.2 us)
Sparse Core Ops, SparseCore 0:
  224.7 70.9 all-reduce.2
where the time goes:
time: 409 us; the launch traced here: 408 us
  starting transfers between devices  111 us (27%)
  waiting for transfers between devices  105 us (26%)
  blocking collectives  102 us (25%)
  other arithmetic  30.2 us (7%)
  local copies, waits for them, and re-layouts  30 us (7%)
  between operations  15 us (4%)
  matrix products  13.8 us (3%)
    psum x1, blocking collectives, local(): log_amp, embed_grad = lax.psum((amp_part, contrib), ('state', 'lat'))  102 us
    psum x1, waiting for transfers between devices, local(): block_grad = lax.psum(own_rows, 'lat')  69 us
    ppermute x10, starting transfers between devices, swapped(): return lax.ppermute(value, axis, pairs)  46.8 us
    ppermute x5, starting transfers between devices, extended(): lax.ppermute(lax.slice_in_dim(block, block.shape[dim] - width, None, axis...  32.6 us
    ppermute x5, starting transfers between devices, extended(): lax.ppermute(lax.slice_in_dim(block, 0, width, axis=dim), axis, backward)  32 us
    ppermute x10, waiting for transfers between devices, swapped(): return lax.ppermute(value, axis, pairs)  30.8 us
    unnamed x21, other arithmetic  10.9 us
    unnamed x78, local copies, waits for them, and re-layouts  9.08 us
  transfers between devices with their start and end apart: 21, of which 10 were waited for; matrix products, arithmetic and copies ran while one was open for 9% of the time, Pallas kernels for 0%

commit v1 on v0

v1 whole, which is shorter than its diff:
```python
import functools
import math

import jax
import jax.numpy as jnp
from jax import lax
from jax.experimental import pallas as pl
from jax.experimental.pallas import tpu as pltpu
from jax.sharding import Mesh
from jax.sharding import PartitionSpec as P

C = 64
LX = 8
LY = 128
ROWS = 2 * LX
SITES = ROWS * LY
CHUNK = 24
HEAD = 6
SCALE = 1.0 / math.sqrt(LX * LY)
F32 = jnp.float32
BF16 = jnp.bfloat16


def lanes(row):
    return pl.ds(row * LY, LY)


def neighbour(row, step):
    return (row // LX) * LX + (row % LX + step) % LX


def tap_row(tap):
    return tap if tap < 5 else tap + 3


def store_shifted(ref, row, value):
    ref[0:C, lanes(row)] = pltpu.roll(value, 1, 1).astype(BF16)
    ref[C : 2 * C, lanes(row)] = value.astype(BF16)
    ref[2 * C : 3 * C, lanes(row)] = pltpu.roll(value, LY - 1, 1).astype(BF16)


def store_spread(ref, row, value):
    for step in range(3):
        ref[step * C : (step + 1) * C, lanes(neighbour(row, step - 1))] = value


def gather_rows(ref, row):
    return (
        ref[0:C, lanes(neighbour(row, -1))]
        + ref[C : 2 * C, lanes(row)]
        + ref[2 * C : 3 * C, lanes(neighbour(row, 1))]
    )


def gather_cols(ref, row):
    return (
        pltpu.roll(ref[0:C, lanes(row)], LY - 1, 1)
        + ref[C : 2 * C, lanes(row)]
        + pltpu.roll(ref[2 * C : 3 * C, lanes(row)], 1, 1)
    )


def matmul(left, right_ref, out_ref):
    for start in range(0, SITES, 256):
        cols = pl.ds(start, 256)
        out_ref[:, cols] = jnp.dot(left, right_ref[:, cols], preferred_element_type=F32)


def dot_nt(left, right):
    return lax.dot_general(left, right, (((1,), (1,)), ((), ())), preferred_element_type=F32)


def main_kernel(
    spin_ref,
    embed_ref,
    weight_hbm,
    readout_ref,
    cot_ref,
    out_ref,
    w_ref,
    wf_ref,
    wt_ref,
    patch_ref,
    h_ref,
    hc_ref,
    gc_ref,
    d2_ref,
    d1_ref,
    slope_ref,
    stream_ref,
    y_ref,
    sem,
):
    state = lax.axis_index("yh") * 8 + lax.axis_index("z")
    lat = lax.axis_index("yl") * 2 + lax.axis_index("core")
    first_walker = lat * 4 + lax.axis_index("x")
    copy = pltpu.make_async_copy(weight_hbm.at[state, 0], w_ref, sem)
    copy.start()

    patch_ref[...] = jnp.zeros_like(patch_ref)
    spin = spin_ref[...].astype(F32)
    rolled = (pltpu.roll(spin, 1, 1), spin, pltpu.roll(spin, LY - 1, 1))
    for row in range(ROWS):
        for tap in range(9):
            source = neighbour(row, tap // 3 - 1)
            patch_ref[tap_row(tap) : tap_row(tap) + 1, lanes(row)] = rolled[tap % 3][
                source : source + 1, :
            ]
    embed = embed_ref[...].astype(F32)
    embed16 = jnp.concatenate(
        [embed[:, 0:5], jnp.zeros((C, 3), F32), embed[:, 5:9], jnp.zeros((C, 4), F32)], axis=1
    ).astype(BF16)
    patches = patch_ref[...].astype(BF16)
    h_ref[...] = jnp.dot(embed16, patches, preferred_element_type=F32).astype(BF16).astype(F32)
    for row in range(ROWS):
        store_shifted(hc_ref, row, h_ref[:, lanes(row)])

    pick = lax.broadcasted_iota(jnp.int32, (16, C), 0) == state
    readout = jnp.where(pick, readout_ref[...].astype(F32), 0.0)
    column = jnp.sum(jnp.transpose(readout), axis=1, keepdims=True)
    cot_row = jnp.sum(jnp.where(pick, cot_ref[...], 0.0), axis=0, keepdims=True)
    walker_lane = lax.broadcasted_iota(jnp.int32, (1, C), 1)
    cots = [
        jnp.sum(jnp.where(walker_lane == first_walker + 32 * k, cot_row, 0.0), axis=1, keepdims=True)
        * SCALE
        for k in range(2)
    ]

    copy.wait()
    for block in range(2):
        for step in range(3):
            wf_ref[block, step * C : (step + 1) * C, :] = w_ref[block][:, 192 * step : 192 * step + 192]
        wt_ref[block] = jnp.transpose(wf_ref[block].astype(F32)).astype(BF16)

    matmul(wf_ref[0], hc_ref, y_ref)
    for row in range(ROWS):
        z = gather_rows(y_ref, row)
        sig = 1.0 / (1.0 + jnp.exp(-z))
        slope_ref[:, lanes(row)] = sig * (1.0 + z * (1.0 - sig))
        store_shifted(gc_ref, row, (z * sig).astype(BF16).astype(F32))

    matmul(wf_ref[1], gc_ref, y_ref)
    amps = []
    for half in range(2):
        weight = cots[half] * column
        total = jnp.zeros((C, LY), F32)
        for row in range(half * LX, half * LX + LX):
            u = h_ref[:, lanes(row)] + gather_rows(y_ref, row)
            sig = 1.0 / (1.0 + jnp.exp(-u))
            total = total + u * sig
            d = weight * (sig * (1.0 + u * (1.0 - sig)))
            stream_ref[:, lanes(row)] = d
            store_spread(d2_ref, row, d.astype(BF16))
        amps.append(jnp.sum(jnp.sum(total * column, axis=0, keepdims=True), axis=1, keepdims=True) * SCALE)

    grad_two = dot_nt(d2_ref[...], gc_ref[...])
    matmul(wt_ref[1], d2_ref, y_ref)
    for row in range(ROWS):
        dz = (gather_cols(y_ref, row) * slope_ref[:, lanes(row)]).astype(BF16)
        store_spread(d1_ref, row, dz)

    grad_one = dot_nt(d1_ref[...], hc_ref[...])
    matmul(wt_ref[0], d1_ref, y_ref)
    embed_sum = jnp.zeros((16, C), F32)
    for row in range(ROWS):
        dh = stream_ref[:, lanes(row)] + gather_cols(y_ref, row)
        high = dh.astype(BF16)
        low = (dh - high.astype(F32)).astype(BF16)
        mine = patch_ref[:, lanes(row)].astype(BF16)
        embed_sum = embed_sum + (dot_nt(mine, high) + dot_nt(mine, low))

    lane = lax.broadcasted_iota(jnp.int32, (8, 2 * C), 1)
    sub = lax.broadcasted_iota(jnp.int32, (8, 2 * C), 0)
    small = jnp.concatenate([embed_sum[0:8], embed_sum[8:16]], axis=1)
    for k in range(2):
        small = jnp.where((sub == 5) & (lane == first_walker + 32 * k), amps[k], small)
    thirds = (
        grad_one[:, 0:LY],
        grad_two[:, 0:LY],
        jnp.concatenate([grad_one[:, LY:192], grad_two[:, LY:192]], axis=1),
    )
    for chunk in range(32):
        out_ref[chunk * CHUNK : chunk * CHUNK + 8, :] = small
    for third in range(3):
        for step in range(3):
            for upper in range(2):
                place = HEAD + (third * 3 + step) * 2 + upper
                for quarter in range(4):
                    base = step * C + quarter * 16 + upper * 8
                    out_ref[pl.ds(quarter * 8 * CHUNK + place, 8, stride=CHUNK), :] = thirds[third][
                        base : base + 8, :
                    ]


def final_kernel(grad_ref, small_ref, amp_ref, out_ref, embed_ref):
    amp_ref[...] = small_ref[:, 5, 0:C]
    total = jnp.sum(small_ref[...], axis=0)
    stacked = jnp.concatenate([total[:, 0:C], total[:, C : 2 * C]], axis=0)
    turned = jnp.transpose(stacked)
    embed_ref[:, 0:5] = turned[:, 0:5]
    embed_ref[:, 5:9] = turned[:, 8:12]
    for upper in range(2):
        for step in range(3):
            both = grad_ref[:, HEAD + (6 + step) * 2 + upper, :]
            for block in range(2):
                main = grad_ref[:, HEAD + (block * 3 + step) * 2 + upper, :]
                rest = both[:, block * C : (block + 1) * C]
                out_ref[upper * 8 : upper * 8 + 8, 0, block, step * 192 : step * 192 + 192] = (
                    jnp.concatenate([main, rest], axis=1)
                )


def vmem(count):
    return [pl.BlockSpec(memory_space=pltpu.VMEM) for _ in range(count)]


def local(spins, embed_w, block_w, readout, amp_cot):
    own = jnp.broadcast_to(spins, (8, 1, LY))
    by_z = lax.all_to_all(own, "z", 0, 0, tiled=True)
    doubled = jnp.concatenate([by_z, by_z], axis=0)
    both = lax.all_to_all(doubled, ("yh", "yl", "core"), 0, 0, tiled=True).reshape(ROWS, LY)
    wide = (192, SITES)
    payload = pl.pallas_call(
        main_kernel,
        out_shape=jax.ShapeDtypeStruct((32 * CHUNK, LY), F32),
        in_specs=vmem(2) + [pl.BlockSpec(memory_space=pl.ANY)] + vmem(2),
        out_specs=pl.BlockSpec(memory_space=pltpu.VMEM),
        scratch_shapes=[
            pltpu.VMEM((2, C, 576), BF16),
            pltpu.VMEM((2, 192, 192), BF16),
            pltpu.VMEM((2, 192, 192), BF16),
            pltpu.VMEM((16, SITES), F32),
            pltpu.VMEM((C, SITES), F32),
            pltpu.VMEM(wide, BF16),
            pltpu.VMEM(wide, BF16),
            pltpu.VMEM(wide, BF16),
            pltpu.VMEM(wide, BF16),
            pltpu.VMEM((C, SITES), F32),
            pltpu.VMEM((C, SITES), F32),
            pltpu.VMEM(wide, F32),
            pltpu.SemaphoreType.DMA,
        ],
        name="states",
    )(both, embed_w, block_w, readout, amp_cot)
    parts = lax.all_to_all(payload.reshape(32, CHUNK, LY), ("x", "yl", "core"), 0, 0, tiled=True)
    own_sum = jnp.sum(parts, axis=0)
    grads = lax.all_to_all(
        jnp.broadcast_to(own_sum, (8, CHUNK, LY)), ("yl", "core"), 0, 0, tiled=True
    )
    small = lax.all_to_all(
        jnp.broadcast_to(own_sum[0:8], (16, 8, LY)), ("yh", "z"), 0, 0, tiled=True
    )
    return pl.pallas_call(
        final_kernel,
        out_shape=(
            jax.ShapeDtypeStruct((16, C), F32),
            jax.ShapeDtypeStruct((16, 1, 2, 576), F32),
            jax.ShapeDtypeStruct((C, 9), F32),
        ),
        in_specs=vmem(2),
        out_specs=tuple(vmem(3)),
        name="outputs",
    )(grads, small)


def solution(mesh):
    fine = Mesh(mesh.devices.reshape(2, 8, 4, 4, 2), ("yh", "z", "x", "yl", "core"))
    return jax.shard_map(
        local,
        mesh=fine,
        in_specs=(P(("yh", "z", "x"), ("yl", "core"), None), P(), P(), P(), P()),
        out_specs=(P(), P(("yh", "z", "x"), None, None, None), P()),
        check_vma=False,
    )
```

time: 409 us -> 89.4 us (0.22)
  starting transfers between devices: 111 us -> 9.22 us
  waiting for transfers between devices: 105 us -> 5.56 us
  blocking collectives: 102 us -> 62 us
  other arithmetic: 30.2 us -> 0.64 us
  local copies, waits for them, and re-layouts: 30 us -> 4.09 us
  between operations: 15 us -> 0.66 us
  matrix products: 13.8 us -> 0 us
  Pallas kernels: 0 us -> 6.71 us
    ppermute x20 -> x0, starting transfers between devices: 111 us -> none  [the longest x10 46.8 us: swapped(): return lax.ppermute(value, axis, pairs)]
    psum x1 -> x0, blocking collectives: 102 us -> none  [local(): log_amp, embed_grad = lax.psum((amp_part, contrib), ('state', 'lat'))]
    psum x1 -> x0, waiting for transfers between devices: 69 us -> none  [local(): block_grad = lax.psum(own_rows, 'lat')]
    all_to_all x0 -> x4, blocking collectives: none -> 62 us  [the longest x1 19.2 us: local(): lax.all_to_all(payload.reshape(32, CHUNK, LY), ('x', 'yl', 'core'), 0, 0,...]
    ppermute x20 -> x0, waiting for transfers between devices: 36.3 us -> none  [the longest x10 30.8 us: swapped(): return lax.ppermute(value, axis, pairs)]
    dot_general x17 -> x0, matrix products: 13.8 us -> none  [the longest x5 8.58 us: conv_apply(): jnp.einsum('ok,nkxy->noxy', weight, patches, preferred_element_type=jnp.f...]
    unnamed x21 -> x0, other arithmetic: 10.9 us -> none
    all_to_all x0 -> x1, starting transfers between devices: none -> 9.22 us  [local(): lax.all_to_all(doubled, ('yh', 'yl', 'core'), 0, 0, tiled=True)]
  transfers between devices with their start and end apart: 21 -> 1, of which waited for: 10 -> 1; matrix products, arithmetic and copies ran while one was open for 9% -> 2% of each run, Pallas kernels for 0% -> 0%
where the time goes in v1:
time: 89.4 us; the launch traced here: 88.8 us
  blocking collectives  62 us (69%)
  starting transfers between devices  9.22 us (10%)
  Pallas kernels  6.71 us (8%)
  waiting for transfers between devices  5.56 us (6%)
  local copies, waits for them, and re-layouts  4.09 us (5%)
    all_to_all x1, blocking collectives, local(): lax.all_to_all(payload.reshape(32, CHUNK, LY), ('x', 'yl', 'core'), 0, 0,...  19.2 us
    all_to_all x1, blocking collectives, local(): by_z = lax.all_to_all(own, 'z', 0, 0, tiled=True)  17.2 us
    all_to_all x1, blocking collectives, local(): lax.all_to_all(jnp.broadcast_to(own_sum[0:8], (16, 8, LY)), ('yh', 'z'),...  15.5 us
    all_to_all x1, blocking collectives, local(): lax.all_to_all(jnp.broadcast_to(own_sum, (8, CHUNK, LY)), ('yl', 'core'),...  10 us
    all_to_all x1, starting transfers between devices, local(): lax.all_to_all(doubled, ('yh', 'yl', 'core'), 0, 0, tiled=True)  9.22 us
    all_to_all x1, waiting for transfers between devices, local(): lax.all_to_all(doubled, ('yh', 'yl', 'core'), 0, 0, tiled=True)  5.56 us
    pallas_call x1, Pallas kernels, local(): pl.pallas_call(main_kernel, out_shape=jax.ShapeDtypeStruct((32 * CHUNK, L...  4.96 us
    unnamed x3, local copies, waits for them, and re-layouts  1.98 us
  transfers between devices with their start and end apart: 1, of which 1 were waited for; matrix products, arithmetic and copies ran while one was open for 2% of the time, Pallas kernels for 0%

profile of v1, /device:TPU:1, one launch (start us, length us, event | category | flops | bytes accessed | tf_op | source)
XLA Modules:
  0.0 88.8 jit_solution(702917876190383677)
XLA Ops:
  0.6 0.7 broadcast_in_dim.14
  1.3 17.2 %all_to_all.25 = s32[8,1,128]{2,1,0:T(1,128)S(1)} all-to-all(s32[8,1,128]{2,1,0:T(1,128)S(1)} %broadcast_in_dim.14), channel_id=1, replica_groups=mesh['yh'=2,'z'=8,'x'=4,'yl'=4,'core'=2] {'z'}, dimensions={0} | all-to-all | bytes 8192 | tf_op jit(solution)/shard_map/all_to_all | solution.py:219
  18.5 0.6 pad_add_fusion
  19.1 9.2 %all-to-all-start.1 = ((s32[16,1,128]{2,1,0:T(1,128)}), s32[16,1,128]{2,1,0:T(1,128)S(1)}, u32[]{:S(2)}, u32[]{:S(2)}) async-start(s32[16,1,128]{2,1,0:T(1,128)} %pad_add_fusion), calls=%async_computation.1 | async-start | bytes 16384 | tf_op jit(solution)/shard_map/all_to_all | solution.py:221
  28.3 1.4 %copy.10.embed_ref = bf16[64,9]{1,0:T(8,128)(2,1)} copy(bf16[64,9]{0,1:T(8,128)(2,1)} %param.6) | data formatting | bytes 2304 | tf_op args[1]
  29.7 5.6 %all-to-all-done.1 = s32[16,1,128]{2,1,0:T(1,128)S(1)} async-done(((s32[16,1,128]{2,1,0:T(1,128)}), s32[16,1,128]{2,1,0:T(1,128)S(1)}, u32[]{:S(2)}, u32[]{:S(2)}) %all-to-all-start.1) | async-done | bytes 8224 | tf_op jit(solution)/shard_map/all_to_all | solution.py:221
  35.2 0.0 copy-start
  35.2 0.6 copy-done
  35.8 5.0 %states.1 = f32[768,128]{1,0:T(8,128)} custom-call(s32[16,128]{1,0:T(8,128)} %bitcast.4, bf16[64,9]{1,0:T(8,128)(2,1)} %copy.10.embed_ref, bf16[16,1,2,64,576]{4,3,2,1,0:T(8,128)(2,1)} %weight_hbm.1, bf16[16,64]{1,0:T(8,128)(2,1)} %readout_ref.1, f32[16,64]{1,0:T(8,128)} %cot_ref.1), custom_call_target="tpu_custom_call" | custom-call | tf_op jit(solution)/shard_map/states/pallas_call | solution.py:223
  40.8 19.2 %all_to_all.26 = f32[32,24,128]{2,1,0:T(8,128)S(1)} all-to-all(f32[32,24,128]{2,1,0:T(8,128)} %bitcast.3), channel_id=1, replica_groups=mesh['yh'=2,'z'=8,'x'=4,'yl'=4,'core'=2] {'x','yl','core'}, dimensions={0} | all-to-all | bytes 786432 | tf_op jit(solution)/shard_map/all_to_all | solution.py:245
  60.1 15.5 %all_to_all.27.small_ref = f32[16,8,128]{2,1,0:T(8,128)} all-to-all(f32[16,8,128]{2,1,0:T(8,128)S(1)} %broadcast_in_dim.16), channel_id=1, replica_groups=mesh['yh'=2,'z'=8,'x'=4,'yl'=4,'core'=2] {'yh','z'}, dimensions={0} | all-to-all | bytes 131072 | tf_op jit(solution)/shard_map/all_to_all | solution.py:250
  75.6 10.0 %all_to_all.28.grad_ref = f32[8,24,128]{2,1,0:T(8,128)} all-to-all(f32[8,24,128]{2,1,0:T(8,128)S(1)} %broadcast_in_dim.15), channel_id=1, replica_groups=mesh['yh'=2,'z'=8,'x'=4,'yl'=4,'core'=2] {'yl','core'}, dimensions={0} | all-to-all | bytes 196608 | tf_op jit(solution)/shard_map/all_to_all | solution.py:247
  85.7 1.8 %outputs.1 = (f32[16,64]{1,0:T(8,128)}, f32[16,1,2,576]{3,2,1,0:T(2,128)}, f32[64,9]{1,0:T(8,128)}) custom-call(f32[8,24,128]{2,1,0:T(8,128)} %all_to_all.28.grad_ref, f32[16,8,128]{2,1,0:T(8,128)} %all_to_all.27.small_ref), custom_call_target="tpu_custom_call" | custom-call | tf_op jit(solution)/shard_map/outputs/pallas_call | solution.py:253
  87.4 1.4 %copy.11 = f32[64,9]{0,1:T(8,128)} copy(f32[64,9]{1,0:T(8,128)} %get-tuple-element.8) | data formatting | bytes 4608 | tf_op jit(solution)/shard_map/outputs/pallas_call | solution.py:253
  (4 shorter events, 0.1 us)
Async XLA Ops:
  19.1 16.2 %all-to-all-start.1 = ((s32[16,1,128]{2,1,0:T(1,128)}), s32[16,1,128]{2,1,0:T(1,128)S(1)}, u32[]{:S(2)}, u32[]{:S(2)}) async-start(s32[16,1,128]{2,1,0:T(1,128)} %pad_add_fusion), calls=%async_computation.1 | async-start | bytes 16384 | tf_op jit(solution)/shard_map/all_to_all | solution.py:221
  35.2 0.6 copy-start

commit v2 on v1

--- a/solution.py
+++ b/solution.py
@@ -1,4 +1,3 @@
-import functools
 import math
 
 import jax
@@ -98,7 +97,13 @@
     copy.start()
 
     patch_ref[...] = jnp.zeros_like(patch_ref)
-    spin = spin_ref[...].astype(F32)
+    spin = jnp.concatenate(
+        [
+            spin_ref[pl.ds(pl.multiple_of(lat * LX + 64 * k, LX), LX), :].astype(F32)
+            for k in range(2)
+        ],
+        axis=0,
+    )
     rolled = (pltpu.roll(spin, 1, 1), spin, pltpu.roll(spin, LY - 1, 1))
     for row in range(ROWS):
         for tap in range(9):
@@ -107,8 +112,10 @@
                 source : source + 1, :
             ]
     embed = embed_ref[...].astype(F32)
-    embed16 = jnp.concatenate(
-        [embed[:, 0:5], jnp.zeros((C, 3), F32), embed[:, 5:9], jnp.zeros((C, 4), F32)], axis=1
+    embed16 = jnp.transpose(
+        jnp.concatenate(
+            [embed[0:5], jnp.zeros((3, C), F32), embed[5:9], jnp.zeros((4, C), F32)], axis=0
+        )
     ).astype(BF16)
     patches = patch_ref[...].astype(BF16)
     h_ref[...] = jnp.dot(embed16, patches, preferred_element_type=F32).astype(BF16).astype(F32)
@@ -192,18 +199,23 @@
                     ]
 
 
-def final_kernel(grad_ref, small_ref, amp_ref, out_ref, embed_ref):
-    amp_ref[...] = small_ref[:, 5, 0:C]
-    total = jnp.sum(small_ref[...], axis=0)
-    stacked = jnp.concatenate([total[:, 0:C], total[:, C : 2 * C]], axis=0)
-    turned = jnp.transpose(stacked)
-    embed_ref[:, 0:5] = turned[:, 0:5]
-    embed_ref[:, 5:9] = turned[:, 8:12]
+def final_kernel(all_ref, amp_ref, out_ref, embed_ref):
+    upper_y = lax.axis_index("yh")
+    depth = lax.axis_index("z")
+    total = jnp.zeros((8, 2 * C), F32)
+    for source in range(16):
+        rows = all_ref[source, 0:8, :]
+        total = total + rows
+        plane = (source // 8) * 8 + lax.rem(depth - source % 8 + 8, 8)
+        amp_ref[pl.ds(plane, 1), :] = rows[5:6, 0:C]
+    embed_ref[0:5, :] = total[0:5, 0:C]
+    embed_ref[5:9, :] = total[0:4, C : 2 * C]
+    base = upper_y * 8
     for upper in range(2):
         for step in range(3):
-            both = grad_ref[:, HEAD + (6 + step) * 2 + upper, :]
+            both = all_ref[pl.ds(base, 8), HEAD + (6 + step) * 2 + upper, :]
             for block in range(2):
-                main = grad_ref[:, HEAD + (block * 3 + step) * 2 + upper, :]
+                main = all_ref[pl.ds(base, 8), HEAD + (block * 3 + step) * 2 + upper, :]
                 rest = both[:, block * C : (block + 1) * C]
                 out_ref[upper * 8 : upper * 8 + 8, 0, block, step * 192 : step * 192 + 192] = (
                     jnp.concatenate([main, rest], axis=1)
@@ -214,11 +226,19 @@
     return [pl.BlockSpec(memory_space=pltpu.VMEM) for _ in range(count)]
 
 
+def shift_pairs():
+    pairs = []
+    for high in range(2):
+        for z in range(8):
+            for rest in range(32):
+                target = (z + rest % 8) % 8
+                pairs.append(((high * 8 + z) * 32 + rest, (high * 8 + target) * 32 + rest))
+    return pairs
+
+
 def local(spins, embed_w, block_w, readout, amp_cot):
-    own = jnp.broadcast_to(spins, (8, 1, LY))
-    by_z = lax.all_to_all(own, "z", 0, 0, tiled=True)
-    doubled = jnp.concatenate([by_z, by_z], axis=0)
-    both = lax.all_to_all(doubled, ("yh", "yl", "core"), 0, 0, tiled=True).reshape(ROWS, LY)
+    own = jnp.broadcast_to(spins, (128, 1, LY))
+    fields = lax.all_to_all(own, ("yh", "z", "yl", "core"), 0, 0, tiled=True).reshape(128, LY)
     wide = (192, SITES)
     payload = pl.pallas_call(
         main_kernel,
@@ -241,26 +261,27 @@
             pltpu.SemaphoreType.DMA,
         ],
         name="states",
-    )(both, embed_w, block_w, readout, amp_cot)
+    )(fields, embed_w.T, block_w, readout, amp_cot)
     parts = lax.all_to_all(payload.reshape(32, CHUNK, LY), ("x", "yl", "core"), 0, 0, tiled=True)
     own_sum = jnp.sum(parts, axis=0)
-    grads = lax.all_to_all(
-        jnp.broadcast_to(own_sum, (8, CHUNK, LY)), ("yl", "core"), 0, 0, tiled=True
-    )
-    small = lax.all_to_all(
-        jnp.broadcast_to(own_sum[0:8], (16, 8, LY)), ("yh", "z"), 0, 0, tiled=True
-    )
-    return pl.pallas_call(
+    shifted = lax.ppermute(own_sum, ("yh", "z", "x", "yl", "core"), shift_pairs())
+    is_small = lax.broadcasted_iota(jnp.int32, (CHUNK, LY), 0) < HEAD
+    mixed = jnp.where(is_small, shifted, own_sum)
+    gathered = lax.all_to_all(
+        jnp.broadcast_to(mixed, (16, CHUNK, LY)), ("yh", "yl", "core"), 0, 0, tiled=True
+    )
+    log_amp, block_grad, embed_grad = pl.pallas_call(
         final_kernel,
         out_shape=(
             jax.ShapeDtypeStruct((16, C), F32),
             jax.ShapeDtypeStruct((16, 1, 2, 576), F32),
-            jax.ShapeDtypeStruct((C, 9), F32),
+            jax.ShapeDtypeStruct((9, C), F32),
         ),
-        in_specs=vmem(2),
+        in_specs=vmem(1),
         out_specs=tuple(vmem(3)),
         name="outputs",
-    )(grads, small)
+    )(gathered)
+    return log_amp, block_grad, embed_grad.T
 
 
 def solution(mesh):

time: 89.4 us -> 80.8 us (0.904)
  starting transfers between devices: 9.22 us -> 2.64 us
  blocking collectives: 62 us -> 66.6 us
  local copies, waits for them, and re-layouts: 4.09 us -> 0.71 us
  waiting for transfers between devices: 5.56 us -> 2.99 us
    all_to_all x1 -> x0, starting transfers between devices: 9.22 us -> none  [local(): lax.all_to_all(doubled, ('yh', 'yl', 'core'), 0, 0, tiled=True)]
    all_to_all x1 -> x0, waiting for transfers between devices: 5.56 us -> none  [local(): lax.all_to_all(doubled, ('yh', 'yl', 'core'), 0, 0, tiled=True)]
    all_to_all x3 -> x2, blocking collectives: 42.8 us -> 46.8 us  [the longest x1 30 us: local(): lax.all_to_all(own, ('yh', 'z', 'yl', 'core'), 0, 0, tiled=True)]
    ppermute x0 -> x1, waiting for transfers between devices: none -> 2.99 us  [local(): lax.ppermute(own_sum, ('yh', 'z', 'x', 'yl', 'core'), shift_pairs())]
    ppermute x0 -> x1, starting transfers between devices: none -> 2.64 us  [local(): lax.ppermute(own_sum, ('yh', 'z', 'x', 'yl', 'core'), shift_pairs())]
    unnamed x3 -> x0, local copies, waits for them, and re-layouts: 1.98 us -> none
    pallas_call x1 -> x0, local copies, waits for them, and re-layouts: 1.43 us -> none  [local(): pl.pallas_call(final_kernel, out_shape=(jax.ShapeDtypeStruct((16, C), F32...]
  transfers between devices with their start and end apart: 1 -> 1, of which waited for: 1 -> 1; matrix products, arithmetic and copies ran while one was open for 2% -> 0% of each run, Pallas kernels for 0% -> 0%
where the time goes in v2:
time: 80.8 us; the launch traced here: 80.5 us
  blocking collectives  66.6 us (82%)
  Pallas kernels  6.79 us (8%)
  waiting for transfers between devices  2.99 us (4%)
  starting transfers between devices  2.64 us (3%)
    all_to_all x1, blocking collectives, local(): lax.all_to_all(own, ('yh', 'z', 'yl', 'core'), 0, 0, tiled=True)  30 us
    all_to_all x1, blocking collectives, local(): lax.all_to_all(payload.reshape(32, CHUNK, LY), ('x', 'yl', 'core'), 0, 0,...  19.8 us
    all_to_all x1, blocking collectives, local(): lax.all_to_all(jnp.broadcast_to(mixed, (16, CHUNK, LY)), ('yh', 'yl', 'co...  16.8 us
    pallas_call x1, Pallas kernels, local(): pl.pallas_call(main_kernel, out_shape=jax.ShapeDtypeStruct((32 * CHUNK, L...  5.06 us
    ppermute x1, waiting for transfers between devices, local(): lax.ppermute(own_sum, ('yh', 'z', 'x', 'yl', 'core'), shift_pairs())  2.99 us
    ppermute x1, starting transfers between devices, local(): lax.ppermute(own_sum, ('yh', 'z', 'x', 'yl', 'core'), shift_pairs())  2.64 us
    pallas_call x1, Pallas kernels, local(): pl.pallas_call(final_kernel, out_shape=(jax.ShapeDtypeStruct((16, C), F32...  1.73 us
  transfers between devices with their start and end apart: 1, of which 1 were waited for; matrix products, arithmetic and copies ran while one was open for 0% of the time, Pallas kernels for 0%

profile of v2, /device:TPU:1, one launch (start us, length us, event | category | flops | bytes accessed | tf_op | source)
XLA Modules:
  0.0 80.5 jit_solution(7245829437242888871)
XLA Ops:
  0.6 0.7 broadcast_in_dim.11
  1.3 30.0 %all_to_all.15 = s32[128,1,128]{2,1,0:T(1,128)} all-to-all(s32[128,1,128]{2,1,0:T(1,128)S(1)} %broadcast_in_dim.11), channel_id=1, replica_groups=mesh['yh'=2,'z'=8,'x'=4,'yl'=4,'core'=2] {'yh','z','yl','core'}, dimensions={0} | all-to-all | bytes 131072 | tf_op jit(solution)/shard_map/all_to_all | solution.py:241
  31.3 5.1 %states.1 = f32[768,128]{1,0:T(8,128)} custom-call(s32[128,128]{1,0:T(8,128)} %bitcast.6, bf16[9,64]{1,0:T(8,128)(2,1)} %bitcast.7, bf16[16,1,2,64,576]{4,3,2,1,0:T(8,128)(2,1)} %weight_hbm.1, bf16[16,64]{1,0:T(8,128)(2,1)} %readout_ref.1, f32[16,64]{1,0:T(8,128)} %cot_ref.1), custom_call_target="tpu_custom_call" | custom-call | tf_op jit(solution)/shard_map/states/pallas_call | solution.py:243
  36.4 19.8 %all_to_all.16 = f32[32,24,128]{2,1,0:T(8,128)S(1)} all-to-all(f32[32,24,128]{2,1,0:T(8,128)} %bitcast.5), channel_id=1, replica_groups=mesh['yh'=2,'z'=8,'x'=4,'yl'=4,'core'=2] {'x','yl','core'}, dimensions={0} | all-to-all | bytes 786432 | tf_op jit(solution)/shard_map/all_to_all | solution.py:265
  56.2 2.6 %collective-permute-start = (f32[24,128]{1,0:T(8,128)S(1)}, f32[24,128]{1,0:T(8,128)S(1)}, u32[]{:S(2)}, u32[]{:S(2)}) collective-permute-start(f32[24,128]{1,0:T(8,128)S(1)} %reduce_sum.9), channel_id=1, source_target_pairs={{0,0},{1,33},{2,66},{3,99},{4,132},{5,165},{6,198},{7,231},{8,8},{... | collective-permute-start | bytes 36872 | tf_op jit(solution)/shard_map/ppermute | solution.py:267
  58.9 3.0 %collective-permute-done = f32[24,128]{1,0:T(8,128)S(1)} collective-permute-done((f32[24,128]{1,0:T(8,128)S(1)}, f32[24,128]{1,0:T(8,128)S(1)}, u32[]{:S(2)}, u32[]{:S(2)}) %collective-permute-start) | collective-permute-done | bytes 12320 | tf_op jit(solution)/shard_map/ppermute | solution.py:267
  61.9 0.1 broadcast_select_fusion
  62.0 16.8 %all_to_all.17.all_ref = f32[16,24,128]{2,1,0:T(8,128)} all-to-all(f32[16,24,128]{2,1,0:T(8,128)S(1)} %broadcast_in_dim.12), channel_id=1, replica_groups=mesh['yh'=2,'z'=8,'x'=4,'yl'=4,'core'=2] {'yh','yl','core'}, dimensions={0} | all-to-all | bytes 393216 | tf_op jit(solution)/shard_map/all_to_all | solution.py:270
  78.7 1.7 %outputs.1 = (f32[16,64]{1,0:T(8,128)}, f32[16,1,2,576]{3,2,1,0:T(2,128)}, f32[9,64]{1,0:T(8,128)}) custom-call(f32[16,24,128]{2,1,0:T(8,128)} %all_to_all.17.all_ref), custom_call_target="tpu_custom_call" | custom-call | tf_op jit(solution)/shard_map/outputs/pallas_call | solution.py:273
  (3 shorter events, 0.1 us)
Async XLA Ops:
  56.2 5.7 %collective-permute-start = (f32[24,128]{1,0:T(8,128)S(1)}, f32[24,128]{1,0:T(8,128)S(1)}, u32[]{:S(2)}, u32[]{:S(2)}) collective-permute-start(f32[24,128]{1,0:T(8,128)S(1)} %reduce_sum.9), channel_id=1, source_target_pairs={{0,0},{1,33},{2,66},{3,99},{4,132},{5,165},{6,198},{7,231},{8,8},{... | collective-permute-start | bytes 36872 | tf_op jit(solution)/shard_map/ppermute | solution.py:267

commit v3 on v2

--- a/solution.py
+++ b/solution.py
@@ -90,20 +90,14 @@
     y_ref,
     sem,
 ):
-    state = lax.axis_index("yh") * 8 + lax.axis_index("z")
-    lat = lax.axis_index("yl") * 2 + lax.axis_index("core")
-    first_walker = lat * 4 + lax.axis_index("x")
+    along = lax.axis_index("yl")
+    state = lax.axis_index("yh") * 8 + jnp.where(lax.axis_index("core") == 0, along, 7 - along)
+    first_walker = lax.axis_index("z") * 4 + lax.axis_index("x")
     copy = pltpu.make_async_copy(weight_hbm.at[state, 0], w_ref, sem)
     copy.start()
 
     patch_ref[...] = jnp.zeros_like(patch_ref)
-    spin = jnp.concatenate(
-        [
-            spin_ref[pl.ds(pl.multiple_of(lat * LX + 64 * k, LX), LX), :].astype(F32)
-            for k in range(2)
-        ],
-        axis=0,
-    )
+    spin = spin_ref[...].astype(F32)
     rolled = (pltpu.roll(spin, 1, 1), spin, pltpu.roll(spin, LY - 1, 1))
     for row in range(ROWS):
         for tap in range(9):
@@ -194,51 +188,60 @@
                 place = HEAD + (third * 3 + step) * 2 + upper
                 for quarter in range(4):
                     base = step * C + quarter * 16 + upper * 8
-                    out_ref[pl.ds(quarter * 8 * CHUNK + place, 8, stride=CHUNK), :] = thirds[third][
+                    out_ref[pl.ds(quarter * CHUNK + place, 8, stride=4 * CHUNK), :] = thirds[third][
                         base : base + 8, :
                     ]
 
 
 def final_kernel(all_ref, amp_ref, out_ref, embed_ref):
-    upper_y = lax.axis_index("yh")
-    depth = lax.axis_index("z")
     total = jnp.zeros((8, 2 * C), F32)
     for source in range(16):
         rows = all_ref[source, 0:8, :]
         total = total + rows
-        plane = (source // 8) * 8 + lax.rem(depth - source % 8 + 8, 8)
-        amp_ref[pl.ds(plane, 1), :] = rows[5:6, 0:C]
+        state = (source // 8) * 8 + folded(source % 8)
+        amp_ref[state : state + 1, :] = rows[5:6, 0:C]
     embed_ref[0:5, :] = total[0:5, 0:C]
     embed_ref[5:9, :] = total[0:4, C : 2 * C]
-    base = upper_y * 8
+    base = lax.axis_index("yh") * 8
     for upper in range(2):
         for step in range(3):
             both = all_ref[pl.ds(base, 8), HEAD + (6 + step) * 2 + upper, :]
             for block in range(2):
                 main = all_ref[pl.ds(base, 8), HEAD + (block * 3 + step) * 2 + upper, :]
                 rest = both[:, block * C : (block + 1) * C]
-                out_ref[upper * 8 : upper * 8 + 8, 0, block, step * 192 : step * 192 + 192] = (
-                    jnp.concatenate([main, rest], axis=1)
-                )
+                value = jnp.concatenate([main, rest], axis=1)
+                for source in range(8):
+                    place = upper * 8 + (folded(source) + 4) % 8
+                    out_ref[place : place + 1, 0, block, step * 192 : step * 192 + 192] = value[
+                        source : source + 1
+                    ]
 
 
 def vmem(count):
     return [pl.BlockSpec(memory_space=pltpu.VMEM) for _ in range(count)]
 
 
-def shift_pairs():
+def folded(lat):
+    along, core = divmod(lat, 2)
+    return 7 - along if core else along
+
+
+def turn_pairs():
     pairs = []
     for high in range(2):
         for z in range(8):
-            for rest in range(32):
-                target = (z + rest % 8) % 8
-                pairs.append(((high * 8 + z) * 32 + rest, (high * 8 + target) * 32 + rest))
+            for x in range(4):
+                for lat in range(8):
+                    place = next(k for k in range(8) if folded(k) == (z + 4) % 8)
+                    source = ((high * 8 + z) * 4 + x) * 8 + lat
+                    target = ((high * 8 + folded(lat)) * 4 + x) * 8 + place
+                    pairs.append((source, target))
     return pairs
 
 
 def local(spins, embed_w, block_w, readout, amp_cot):
-    own = jnp.broadcast_to(spins, (128, 1, LY))
-    fields = lax.all_to_all(own, ("yh", "z", "yl", "core"), 0, 0, tiled=True).reshape(128, LY)
+    own = jnp.broadcast_to(spins, (16, 1, LY))
+    fields = lax.all_to_all(own, ("yh", "yl", "core"), 0, 0, tiled=True).reshape(ROWS, LY)
     wide = (192, SITES)
     payload = pl.pallas_call(
         main_kernel,
@@ -262,11 +265,11 @@
         ],
         name="states",
     )(fields, embed_w.T, block_w, readout, amp_cot)
-    parts = lax.all_to_all(payload.reshape(32, CHUNK, LY), ("x", "yl", "core"), 0, 0, tiled=True)
+    parts = lax.all_to_all(payload.reshape(32, CHUNK, LY), ("z", "x"), 0, 0, tiled=True)
     own_sum = jnp.sum(parts, axis=0)
-    shifted = lax.ppermute(own_sum, ("yh", "z", "x", "yl", "core"), shift_pairs())
+    turned = lax.ppermute(own_sum, ("yh", "z", "x", "yl", "core"), turn_pairs())
     is_small = lax.broadcasted_iota(jnp.int32, (CHUNK, LY), 0) < HEAD
-    mixed = jnp.where(is_small, shifted, own_sum)
+    mixed = jnp.where(is_small, own_sum, turned)
     gathered = lax.all_to_all(
         jnp.broadcast_to(mixed, (16, CHUNK, LY)), ("yh", "yl", "core"), 0, 0, tiled=True
     )

time: 80.8 us -> 76.2 us (0.943)
  blocking collectives: 66.6 us -> 60.7 us
  waiting for transfers between devices: 2.99 us -> 4.94 us
    all_to_all x2, blocking collectives: 49.8 us -> 42.2 us  [the longest x1 25.3 us: local(): lax.all_to_all(payload.reshape(32, CHUNK, LY), ('z', 'x'), 0, 0, tiled=True)]
    ppermute x1, waiting for transfers between devices: 2.99 us -> 4.94 us  [local(): turned = lax.ppermute(own_sum, ('yh', 'z', 'x', 'yl', 'core'), turn_pairs())]
    all_to_all x1, blocking collectives: 16.8 us -> 18.6 us  [local(): lax.all_to_all(jnp.broadcast_to(mixed, (16, CHUNK, LY)), ('yh', 'yl', 'co...]
where the time goes in v3:
time: 76.2 us; the launch traced here: 75.8 us
  blocking collectives  60.7 us (80%)
  Pallas kernels  6.76 us (9%)
  waiting for transfers between devices  4.94 us (6%)
  starting transfers between devices  1.92 us (3%)
    all_to_all x1, blocking collectives, local(): lax.all_to_all(payload.reshape(32, CHUNK, LY), ('z', 'x'), 0, 0, tiled=True)  25.3 us
    all_to_all x1, blocking collectives, local(): lax.all_to_all(jnp.broadcast_to(mixed, (16, CHUNK, LY)), ('yh', 'yl', 'co...  18.6 us
    all_to_all x1, blocking collectives, local(): lax.all_to_all(own, ('yh', 'yl', 'core'), 0, 0, tiled=True)  16.8 us
    pallas_call x1, Pallas kernels, local(): pl.pallas_call(main_kernel, out_shape=jax.ShapeDtypeStruct((32 * CHUNK, L...  5.03 us
    ppermute x1, waiting for transfers between devices, local(): turned = lax.ppermute(own_sum, ('yh', 'z', 'x', 'yl', 'core'), turn_pairs())  4.94 us
    ppermute x1, starting transfers between devices, local(): turned = lax.ppermute(own_sum, ('yh', 'z', 'x', 'yl', 'core'), turn_pairs())  1.92 us
    pallas_call x1, Pallas kernels, local(): pl.pallas_call(final_kernel, out_shape=(jax.ShapeDtypeStruct((16, C), F32...  1.73 us
  transfers between devices with their start and end apart: 1, of which 1 were waited for; matrix products, arithmetic and copies ran while one was open for 0% of the time, Pallas kernels for 0%

profile of v3, /device:TPU:1, one launch (start us, length us, event | category | flops | bytes accessed | tf_op | source)
XLA Modules:
  0.0 75.8 jit_solution(10177896239862648740)
XLA Ops:
  0.6 0.7 broadcast_in_dim.11
  1.3 16.8 %all_to_all.15 = s32[16,1,128]{2,1,0:T(1,128)} all-to-all(s32[16,1,128]{2,1,0:T(1,128)S(1)} %broadcast_in_dim.11), channel_id=1, replica_groups=mesh['yh'=2,'z'=8,'x'=4,'yl'=4,'core'=2] {'yh','yl','core'}, dimensions={0} | all-to-all | bytes 16384 | tf_op jit(solution)/shard_map/all_to_all | solution.py:244
  18.1 5.0 %states.1 = f32[768,128]{1,0:T(8,128)} custom-call(s32[16,128]{1,0:T(8,128)} %bitcast.6, bf16[9,64]{1,0:T(8,128)(2,1)} %bitcast.7, bf16[16,1,2,64,576]{4,3,2,1,0:T(8,128)(2,1)} %weight_hbm.1, bf16[16,64]{1,0:T(8,128)(2,1)} %readout_ref.1, f32[16,64]{1,0:T(8,128)} %cot_ref.1), custom_call_target="tpu_custom_call" | custom-call | tf_op jit(solution)/shard_map/states/pallas_call | solution.py:246
  23.2 25.3 %all_to_all.16 = f32[32,24,128]{2,1,0:T(8,128)S(1)} all-to-all(f32[32,24,128]{2,1,0:T(8,128)} %bitcast.5), channel_id=1, replica_groups=mesh['yh'=2,'z'=8,'x'=4,'yl'=4,'core'=2] {'z','x'}, dimensions={0} | all-to-all | bytes 786432 | tf_op jit(solution)/shard_map/all_to_all | solution.py:268
  48.5 1.9 %collective-permute-start = (f32[24,128]{1,0:T(8,128)S(1)}, f32[24,128]{1,0:T(8,128)S(1)}, u32[]{:S(2)}, u32[]{:S(2)}) collective-permute-start(f32[24,128]{1,0:T(8,128)S(1)} %reduce_sum.9), channel_id=1, source_target_pairs={{0,7},{1,231},{2,39},{3,199},{4,71},{5,167},{6,103},{7,135},{8,15}... | collective-permute-start | bytes 36872 | tf_op jit(solution)/shard_map/ppermute | solution.py:270
  50.5 4.9 %collective-permute-done = f32[24,128]{1,0:T(8,128)S(1)} collective-permute-done((f32[24,128]{1,0:T(8,128)S(1)}, f32[24,128]{1,0:T(8,128)S(1)}, u32[]{:S(2)}, u32[]{:S(2)}) %collective-permute-start) | collective-permute-done | bytes 12320 | tf_op jit(solution)/shard_map/ppermute | solution.py:270
  55.4 0.1 broadcast_select_fusion
  55.5 18.6 %all_to_all.17.all_ref = f32[16,24,128]{2,1,0:T(8,128)} all-to-all(f32[16,24,128]{2,1,0:T(8,128)S(1)} %broadcast_in_dim.12), channel_id=1, replica_groups=mesh['yh'=2,'z'=8,'x'=4,'yl'=4,'core'=2] {'yh','yl','core'}, dimensions={0} | all-to-all | bytes 393216 | tf_op jit(solution)/shard_map/all_to_all | solution.py:273
  74.1 1.7 %outputs.1 = (f32[16,64]{1,0:T(8,128)}, f32[16,1,2,576]{3,2,1,0:T(2,128)}, f32[9,64]{1,0:T(8,128)}) custom-call(f32[16,24,128]{2,1,0:T(8,128)} %all_to_all.17.all_ref), custom_call_target="tpu_custom_call" | custom-call | tf_op jit(solution)/shard_map/outputs/pallas_call | solution.py:276
  (3 shorter events, 0.1 us)
Async XLA Ops:
  48.5 6.9 %collective-permute-start = (f32[24,128]{1,0:T(8,128)S(1)}, f32[24,128]{1,0:T(8,128)S(1)}, u32[]{:S(2)}, u32[]{:S(2)}) collective-permute-start(f32[24,128]{1,0:T(8,128)S(1)} %reduce_sum.9), channel_id=1, source_target_pairs={{0,7},{1,231},{2,39},{3,199},{4,71},{5,167},{6,103},{7,135},{8,15}... | collective-permute-start | bytes 36872 | tf_op jit(solution)/shard_map/ppermute | solution.py:270

commit v4 on v3

--- a/solution.py
+++ b/solution.py
@@ -28,14 +28,10 @@
     return (row // LX) * LX + (row % LX + step) % LX
 
 
-def tap_row(tap):
-    return tap if tap < 5 else tap + 3
-
-
 def store_shifted(ref, row, value):
-    ref[0:C, lanes(row)] = pltpu.roll(value, 1, 1).astype(BF16)
-    ref[C : 2 * C, lanes(row)] = value.astype(BF16)
-    ref[2 * C : 3 * C, lanes(row)] = pltpu.roll(value, LY - 1, 1).astype(BF16)
+    ref[0:C, lanes(row)] = pltpu.roll(value, 1, 1)
+    ref[C : 2 * C, lanes(row)] = value
+    ref[2 * C : 3 * C, lanes(row)] = pltpu.roll(value, LY - 1, 1)
 
 
 def store_spread(ref, row, value):
@@ -59,14 +55,18 @@
     )
 
 
-def matmul(left, right_ref, out_ref):
-    for start in range(0, SITES, 256):
+def matmul(left, right_ref, out_ref, half):
+    for start in range(half * SITES // 2, (half + 1) * SITES // 2, 256):
         cols = pl.ds(start, 256)
         out_ref[:, cols] = jnp.dot(left, right_ref[:, cols], preferred_element_type=F32)
 
 
 def dot_nt(left, right):
     return lax.dot_general(left, right, (((1,), (1,)), ((), ())), preferred_element_type=F32)
+
+
+def sigmoid(v):
+    return 1.0 / (1.0 + jnp.exp(-v))
 
 
 def main_kernel(
@@ -79,6 +79,7 @@
     w_ref,
     wf_ref,
     wt_ref,
+    pad_ref,
     patch_ref,
     h_ref,
     hc_ref,
@@ -87,7 +88,9 @@
     d1_ref,
     slope_ref,
     stream_ref,
-    y_ref,
+    ya_ref,
+    yb_ref,
+    parts_ref,
     sem,
 ):
     along = lax.axis_index("yl")
@@ -95,26 +98,32 @@
     first_walker = lax.axis_index("z") * 4 + lax.axis_index("x")
     copy = pltpu.make_async_copy(weight_hbm.at[state, 0], w_ref, sem)
     copy.start()
-
-    patch_ref[...] = jnp.zeros_like(patch_ref)
+    halves = [range(half * LX, half * LX + LX) for half in range(2)]
+
     spin = spin_ref[...].astype(F32)
-    rolled = (pltpu.roll(spin, 1, 1), spin, pltpu.roll(spin, LY - 1, 1))
-    for row in range(ROWS):
-        for tap in range(9):
-            source = neighbour(row, tap // 3 - 1)
-            patch_ref[tap_row(tap) : tap_row(tap) + 1, lanes(row)] = rolled[tap % 3][
-                source : source + 1, :
-            ]
+    for half in range(2):
+        turned = pltpu.roll(spin[half * LX : half * LX + LX], 1, 0)
+        for step, value in enumerate((pltpu.roll(turned, 1, 1), turned, pltpu.roll(turned, LY - 1, 1))):
+            pad_ref[step, half * 16 : half * 16 + 8] = value
+            pad_ref[step, half * 16 + 8 : half * 16 + 16] = value
     embed = embed_ref[...].astype(F32)
-    embed16 = jnp.transpose(
-        jnp.concatenate(
-            [embed[0:5], jnp.zeros((3, C), F32), embed[5:9], jnp.zeros((4, C), F32)], axis=0
-        )
-    ).astype(BF16)
-    patches = patch_ref[...].astype(BF16)
-    h_ref[...] = jnp.dot(embed16, patches, preferred_element_type=F32).astype(BF16).astype(F32)
-    for row in range(ROWS):
-        store_shifted(hc_ref, row, h_ref[:, lanes(row)])
+    nothing = jnp.zeros((5, C), F32)
+    rows = []
+    for step in range(3):
+        rows += [embed[3 * k + step : 3 * k + step + 1] for k in range(3)] + [nothing]
+    embed24 = jnp.transpose(jnp.concatenate(rows, axis=0)).astype(BF16)
+    for half in range(2):
+        for row in halves[half]:
+            first = half * 16 + row % LX
+            patch_ref[:, lanes(row)] = jnp.concatenate(
+                [pad_ref[step, first : first + 8] for step in range(3)], axis=0
+            ).astype(BF16)
+        for row in halves[half]:
+            value = jnp.dot(
+                embed24, patch_ref[:, lanes(row)], preferred_element_type=F32
+            ).astype(BF16)
+            h_ref[:, lanes(row)] = value.astype(F32)
+            store_shifted(hc_ref, row, value)
 
     pick = lax.broadcasted_iota(jnp.int32, (16, C), 0) == state
     readout = jnp.where(pick, readout_ref[...].astype(F32), 0.0)
@@ -133,48 +142,68 @@
             wf_ref[block, step * C : (step + 1) * C, :] = w_ref[block][:, 192 * step : 192 * step + 192]
         wt_ref[block] = jnp.transpose(wf_ref[block].astype(F32)).astype(BF16)
 
-    matmul(wf_ref[0], hc_ref, y_ref)
-    for row in range(ROWS):
-        z = gather_rows(y_ref, row)
-        sig = 1.0 / (1.0 + jnp.exp(-z))
-        slope_ref[:, lanes(row)] = sig * (1.0 + z * (1.0 - sig))
-        store_shifted(gc_ref, row, (z * sig).astype(BF16).astype(F32))
-
-    matmul(wf_ref[1], gc_ref, y_ref)
-    amps = []
-    for half in range(2):
+    def first_act(half):
+        for row in halves[half]:
+            z = gather_rows(ya_ref, row)
+            sig = sigmoid(z)
+            slope_ref[:, lanes(row)] = sig * (1.0 + z * (1.0 - sig))
+            store_shifted(gc_ref, row, (z * sig).astype(BF16))
+
+    def second_act(half):
         weight = cots[half] * column
         total = jnp.zeros((C, LY), F32)
-        for row in range(half * LX, half * LX + LX):
-            u = h_ref[:, lanes(row)] + gather_rows(y_ref, row)
-            sig = 1.0 / (1.0 + jnp.exp(-u))
+        for row in halves[half]:
+            u = h_ref[:, lanes(row)] + gather_rows(yb_ref, row)
+            sig = sigmoid(u)
             total = total + u * sig
             d = weight * (sig * (1.0 + u * (1.0 - sig)))
             stream_ref[:, lanes(row)] = d
             store_spread(d2_ref, row, d.astype(BF16))
-        amps.append(jnp.sum(jnp.sum(total * column, axis=0, keepdims=True), axis=1, keepdims=True) * SCALE)
-
+        return (
+            jnp.sum(jnp.sum(total * column, axis=0, keepdims=True), axis=1, keepdims=True) * SCALE
+        )
+
+    def first_back(half):
+        for row in halves[half]:
+            dz = (gather_cols(ya_ref, row) * slope_ref[:, lanes(row)]).astype(BF16)
+            store_spread(d1_ref, row, dz)
+
+    def last_back(half):
+        for row in halves[half]:
+            dh = stream_ref[:, lanes(row)] + gather_cols(yb_ref, row)
+            high = dh.astype(BF16)
+            parts_ref[0:C, lanes(row)] = high
+            parts_ref[C : 2 * C, lanes(row)] = (dh - high.astype(F32)).astype(BF16)
+
+    matmul(wf_ref[0], hc_ref, ya_ref, 0)
+    matmul(wf_ref[0], hc_ref, ya_ref, 1)
+    first_act(0)
+    matmul(wf_ref[1], gc_ref, yb_ref, 0)
+    first_act(1)
+    matmul(wf_ref[1], gc_ref, yb_ref, 1)
+    amps = [second_act(0)]
+    matmul(wt_ref[1], d2_ref, ya_ref, 0)
+    amps.append(second_act(1))
+    matmul(wt_ref[1], d2_ref, ya_ref, 1)
+    first_back(0)
     grad_two = dot_nt(d2_ref[...], gc_ref[...])
-    matmul(wt_ref[1], d2_ref, y_ref)
-    for row in range(ROWS):
-        dz = (gather_cols(y_ref, row) * slope_ref[:, lanes(row)]).astype(BF16)
-        store_spread(d1_ref, row, dz)
-
+    matmul(wt_ref[0], d1_ref, yb_ref, 0)
+    first_back(1)
+    matmul(wt_ref[0], d1_ref, yb_ref, 1)
+    last_back(0)
     grad_one = dot_nt(d1_ref[...], hc_ref[...])
-    matmul(wt_ref[0], d1_ref, y_ref)
-    embed_sum = jnp.zeros((16, C), F32)
-    for row in range(ROWS):
-        dh = stream_ref[:, lanes(row)] + gather_cols(y_ref, row)
-        high = dh.astype(BF16)
-        low = (dh - high.astype(F32)).astype(BF16)
-        mine = patch_ref[:, lanes(row)].astype(BF16)
-        embed_sum = embed_sum + (dot_nt(mine, high) + dot_nt(mine, low))
+    last_back(1)
+    both = dot_nt(parts_ref[...], patch_ref[...])
+    taps = jnp.transpose(both[0:C] + both[C : 2 * C])
 
     lane = lax.broadcasted_iota(jnp.int32, (8, 2 * C), 1)
     sub = lax.broadcasted_iota(jnp.int32, (8, 2 * C), 0)
-    small = jnp.concatenate([embed_sum[0:8], embed_sum[8:16]], axis=1)
+    left = jnp.concatenate([taps[0:3], taps[16:19], jnp.zeros((2, C), F32)], axis=0)
+    right = jnp.concatenate([taps[8:11], jnp.zeros((5, C), F32)], axis=0)
+    small = jnp.concatenate([left, right], axis=1)
     for k in range(2):
-        small = jnp.where((sub == 5) & (lane == first_walker + 32 * k), amps[k], small)
+        here = ((sub == 3) | (sub == 4)) & (lane == C + first_walker + 32 * k)
+        small = jnp.where(here, amps[k], small)
     thirds = (
         grad_one[:, 0:LY],
         grad_two[:, 0:LY],
@@ -194,20 +223,22 @@
 
 
 def final_kernel(all_ref, amp_ref, out_ref, embed_ref):
+    own = lax.axis_index("yh") * 8
     total = jnp.zeros((8, 2 * C), F32)
-    for source in range(16):
+    for source in range(8):
         rows = all_ref[source, 0:8, :]
         total = total + rows
-        state = (source // 8) * 8 + folded(source % 8)
-        amp_ref[state : state + 1, :] = rows[5:6, 0:C]
-    embed_ref[0:5, :] = total[0:5, 0:C]
-    embed_ref[5:9, :] = total[0:4, C : 2 * C]
-    base = lax.axis_index("yh") * 8
+        amp_ref[pl.ds(own + folded(source), 1), :] = rows[3:4, C : 2 * C]
+        amp_ref[pl.ds(8 - own + folded(source), 1), :] = rows[4:5, C : 2 * C]
+    for step in range(3):
+        embed_ref[3 * step : 3 * step + 1, :] = total[step : step + 1, 0:C]
+        embed_ref[3 * step + 1 : 3 * step + 2, :] = total[step : step + 1, C : 2 * C]
+        embed_ref[3 * step + 2 : 3 * step + 3, :] = total[3 + step : 4 + step, 0:C]
     for upper in range(2):
         for step in range(3):
-            both = all_ref[pl.ds(base, 8), HEAD + (6 + step) * 2 + upper, :]
+            both = all_ref[:, HEAD + (6 + step) * 2 + upper, :]
             for block in range(2):
-                main = all_ref[pl.ds(base, 8), HEAD + (block * 3 + step) * 2 + upper, :]
+                main = all_ref[:, HEAD + (block * 3 + step) * 2 + upper, :]
                 rest = both[:, block * C : (block + 1) * C]
                 value = jnp.concatenate([main, rest], axis=1)
                 for source in range(8):
@@ -252,7 +283,8 @@
             pltpu.VMEM((2, C, 576), BF16),
             pltpu.VMEM((2, 192, 192), BF16),
             pltpu.VMEM((2, 192, 192), BF16),
-            pltpu.VMEM((16, SITES), F32),
+            pltpu.VMEM((3, 32, LY), F32),
+            pltpu.VMEM((24, SITES), BF16),
             pltpu.VMEM((C, SITES), F32),
             pltpu.VMEM(wide, BF16),
             pltpu.VMEM(wide, BF16),
@@ -261,6 +293,8 @@
             pltpu.VMEM((C, SITES), F32),
             pltpu.VMEM((C, SITES), F32),
             pltpu.VMEM(wide, F32),
+            pltpu.VMEM(wide, F32),
+            pltpu.VMEM((2 * C, SITES), BF16),
             pltpu.SemaphoreType.DMA,
         ],
         name="states",
@@ -268,10 +302,13 @@
     parts = lax.all_to_all(payload.reshape(32, CHUNK, LY), ("z", "x"), 0, 0, tiled=True)
     own_sum = jnp.sum(parts, axis=0)
     turned = lax.ppermute(own_sum, ("yh", "z", "x", "yl", "core"), turn_pairs())
-    is_small = lax.broadcasted_iota(jnp.int32, (CHUNK, LY), 0) < HEAD
-    mixed = jnp.where(is_small, own_sum, turned)
+    other = lax.ppermute(own_sum, "yh", [(0, 1), (1, 0)])
+    row = lax.broadcasted_iota(jnp.int32, (CHUNK, LY), 0)
+    is_right = lax.broadcasted_iota(jnp.int32, (CHUNK, LY), 1) >= C
+    small = jnp.where(is_right & (row == 3), own_sum, jnp.where(is_right & (row == 4), other, own_sum + other))
+    mixed = jnp.where(row < HEAD, small, turned)
     gathered = lax.all_to_all(
-        jnp.broadcast_to(mixed, (16, CHUNK, LY)), ("yh", "yl", "core"), 0, 0, tiled=True
+        jnp.broadcast_to(mixed, (8, CHUNK, LY)), ("yl", "core"), 0, 0, tiled=True
     )
     log_amp, block_grad, embed_grad = pl.pallas_call(
         final_kernel,

time: 76.2 us -> 75 us (0.984)
  blocking collectives: 60.7 us -> 31.9 us
  starting transfers between devices: 1.92 us -> 17.4 us
  waiting for transfers between devices: 4.94 us -> 17.3 us
    all_to_all x2 -> x1, blocking collectives: 43.9 us -> 14.9 us  [local(): lax.all_to_all(jnp.broadcast_to(mixed, (8, CHUNK, LY)), ('yl', 'core'), 0...]
    all_to_all x0 -> x1, waiting for transfers between devices: none -> 13.8 us  [local(): lax.all_to_all(payload.reshape(32, CHUNK, LY), ('z', 'x'), 0, 0, tiled=True)]
    all_to_all x0 -> x1, starting transfers between devices: none -> 11.4 us  [local(): lax.all_to_all(payload.reshape(32, CHUNK, LY), ('z', 'x'), 0, 0, tiled=True)]
    ppermute x1, waiting for transfers between devices: 4.94 us -> 1 us  [local(): turned = lax.ppermute(own_sum, ('yh', 'z', 'x', 'yl', 'core'), turn_pairs())]
    ppermute x0 -> x1, waiting for transfers between devices: none -> 2.52 us  [local(): other = lax.ppermute(own_sum, 'yh', [(0, 1), (1, 0)])]
    ppermute x0 -> x1, starting transfers between devices: none -> 2.23 us  [local(): other = lax.ppermute(own_sum, 'yh', [(0, 1), (1, 0)])]
    ppermute x1, starting transfers between devices: 1.92 us -> 3.7 us  [local(): turned = lax.ppermute(own_sum, ('yh', 'z', 'x', 'yl', 'core'), turn_pairs())]
  transfers between devices with their start and end apart: 1 -> 3, of which waited for: 1 -> 3; matrix products, arithmetic and copies ran while one was open for 0% -> 0% of each run, Pallas kernels for 0% -> 0%
where the time goes in v4:
time: 75 us; the launch traced here: 74.5 us
  blocking collectives  31.9 us (43%)
  starting transfers between devices  17.4 us (23%)
  waiting for transfers between devices  17.3 us (23%)
  Pallas kernels  6.47 us (9%)
    all_to_all x1, blocking collectives, local(): lax.all_to_all(own, ('yh', 'yl', 'core'), 0, 0, tiled=True)  17 us
    all_to_all x1, blocking collectives, local(): lax.all_to_all(jnp.broadcast_to(mixed, (8, CHUNK, LY)), ('yl', 'core'), 0...  14.9 us
    all_to_all x1, waiting for transfers between devices, local(): lax.all_to_all(payload.reshape(32, CHUNK, LY), ('z', 'x'), 0, 0, tiled=True)  13.8 us
    all_to_all x1, starting transfers between devices, local(): lax.all_to_all(payload.reshape(32, CHUNK, LY), ('z', 'x'), 0, 0, tiled=True)  11.4 us
    pallas_call x1, Pallas kernels, local(): pl.pallas_call(main_kernel, out_shape=jax.ShapeDtypeStruct((32 * CHUNK, L...  4.77 us
    ppermute x1, starting transfers between devices, local(): turned = lax.ppermute(own_sum, ('yh', 'z', 'x', 'yl', 'core'), turn_pairs())  3.7 us
    ppermute x1, waiting for transfers between devices, local(): other = lax.ppermute(own_sum, 'yh', [(0, 1), (1, 0)])  2.52 us
    ppermute x1, starting transfers between devices, local(): other = lax.ppermute(own_sum, 'yh', [(0, 1), (1, 0)])  2.23 us
  transfers between devices with their start and end apart: 3, of which 3 were waited for; matrix products, arithmetic and copies ran while one was open for 0% of the time, Pallas kernels for 0%

profile of v4, /device:TPU:1, one launch (start us, length us, event | category | flops | bytes accessed | tf_op | source)
XLA Modules:
  0.0 74.5 jit_solution(13580821377028638310)
XLA Ops:
  0.6 0.7 broadcast_in_dim.11
  1.3 17.0 %all_to_all.15 = s32[16,1,128]{2,1,0:T(1,128)} all-to-all(s32[16,1,128]{2,1,0:T(1,128)S(1)} %broadcast_in_dim.11), channel_id=1, replica_groups=mesh['yh'=2,'z'=8,'x'=4,'yl'=4,'core'=2] {'yh','yl','core'}, dimensions={0} | all-to-all | bytes 16384 | tf_op jit(solution)/shard_map/all_to_all | solution.py:275
  18.3 4.8 %states.1 = f32[768,128]{1,0:T(8,128)} custom-call(s32[16,128]{1,0:T(8,128)} %bitcast.6, bf16[9,64]{1,0:T(8,128)(2,1)} %bitcast.7, bf16[16,1,2,64,576]{4,3,2,1,0:T(8,128)(2,1)} %weight_hbm.1, bf16[16,64]{1,0:T(8,128)(2,1)} %readout_ref.1, f32[16,64]{1,0:T(8,128)} %cot_ref.1), custom_call_target="tpu_custom_call" | custom-call | tf_op jit(solution)/shard_map/states/pallas_call | solution.py:277
  23.1 11.4 %all-to-all-start.1 = ((f32[32,24,128]{2,1,0:T(8,128)}), f32[32,24,128]{2,1,0:T(8,128)S(1)}, u32[]{:S(2)}, u32[]{:S(2)}) async-start(f32[32,24,128]{2,1,0:T(8,128)} %bitcast.5), calls=%async_computation.1 | async-start | bytes 786432 | tf_op jit(solution)/shard_map/all_to_all | solution.py:302
  34.5 13.8 %all-to-all-done.1 = f32[32,24,128]{2,1,0:T(8,128)S(1)} async-done(((f32[32,24,128]{2,1,0:T(8,128)}), f32[32,24,128]{2,1,0:T(8,128)S(1)}, u32[]{:S(2)}, u32[]{:S(2)}) %all-to-all-start.1) | async-done | bytes 393248 | tf_op jit(solution)/shard_map/all_to_all | solution.py:302
  48.3 2.2 %collective-permute-start = (f32[24,128]{1,0:T(8,128)S(1)}, f32[24,128]{1,0:T(8,128)S(1)}, u32[]{:S(2)}, u32[]{:S(2)}) collective-permute-start(f32[24,128]{1,0:T(8,128)S(1)} %reduce_sum.9), channel_id=1, source_target_pairs={{0,256},{256,0},{1,257},{257,1},{2,258},{258,2},{3,259},{259,3},{4... | collective-permute-start | bytes 36872 | tf_op jit(solution)/shard_map/ppermute | solution.py:305
  50.6 3.7 %collective-permute-start.1 = (f32[24,128]{1,0:T(8,128)S(1)}, f32[24,128]{1,0:T(8,128)S(1)}, u32[]{:S(2)}, u32[]{:S(2)}) collective-permute-start(f32[24,128]{1,0:T(8,128)S(1)} %reduce_sum.9), channel_id=1, source_target_pairs={{0,7},{1,231},{2,39},{3,199},{4,71},{5,167},{6,103},{7,135},{8,15}... | collective-permute-start | bytes 36872 | tf_op jit(solution)/shard_map/ppermute | solution.py:304
  54.3 2.5 %collective-permute-done = f32[24,128]{1,0:T(8,128)S(1)} collective-permute-done((f32[24,128]{1,0:T(8,128)S(1)}, f32[24,128]{1,0:T(8,128)S(1)}, u32[]{:S(2)}, u32[]{:S(2)}) %collective-permute-start) | collective-permute-done | bytes 12320 | tf_op jit(solution)/shard_map/ppermute | solution.py:305
  56.8 1.0 %collective-permute-done.1 = f32[24,128]{1,0:T(8,128)S(1)} collective-permute-done((f32[24,128]{1,0:T(8,128)S(1)}, f32[24,128]{1,0:T(8,128)S(1)}, u32[]{:S(2)}, u32[]{:S(2)}) %collective-permute-start.1) | collective-permute-done | bytes 12320 | tf_op jit(solution)/shard_map/ppermute | solution.py:304
  57.8 0.1 fusion.1
  57.9 14.9 %all_to_all.16.all_ref = f32[8,24,128]{2,1,0:T(8,128)} all-to-all(f32[8,24,128]{2,1,0:T(8,128)S(1)} %broadcast_in_dim.12), channel_id=1, replica_groups=mesh['yh'=2,'z'=8,'x'=4,'yl'=4,'core'=2] {'yl','core'}, dimensions={0} | all-to-all | bytes 196608 | tf_op jit(solution)/shard_map/all_to_all | solution.py:310
  72.8 1.7 %outputs.1 = (f32[16,64]{1,0:T(8,128)}, f32[16,1,2,576]{3,2,1,0:T(2,128)}, f32[9,64]{1,0:T(8,128)}) custom-call(f32[8,24,128]{2,1,0:T(8,128)} %all_to_all.16.all_ref), custom_call_target="tpu_custom_call" | custom-call | tf_op jit(solution)/shard_map/outputs/pallas_call | solution.py:313
  (5 shorter events, 0.1 us)
Async XLA Ops:
  23.1 25.2 %all-to-all-start.1 = ((f32[32,24,128]{2,1,0:T(8,128)}), f32[32,24,128]{2,1,0:T(8,128)S(1)}, u32[]{:S(2)}, u32[]{:S(2)}) async-start(f32[32,24,128]{2,1,0:T(8,128)} %bitcast.5), calls=%async_computation.1 | async-start | bytes 786432 | tf_op jit(solution)/shard_map/all_to_all | solution.py:302
  48.3 8.5 %collective-permute-start = (f32[24,128]{1,0:T(8,128)S(1)}, f32[24,128]{1,0:T(8,128)S(1)}, u32[]{:S(2)}, u32[]{:S(2)}) collective-permute-start(f32[24,128]{1,0:T(8,128)S(1)} %reduce_sum.9), channel_id=1, source_target_pairs={{0,256},{256,0},{1,257},{257,1},{2,258},{258,2},{3,259},{259,3},{4... | collective-permute-start | bytes 36872 | tf_op jit(solution)/shard_map/ppermute | solution.py:305
  50.6 7.2 %collective-permute-start.1 = (f32[24,128]{1,0:T(8,128)S(1)}, f32[24,128]{1,0:T(8,128)S(1)}, u32[]{:S(2)}, u32[]{:S(2)}) collective-permute-start(f32[24,128]{1,0:T(8,128)S(1)} %reduce_sum.9), channel_id=1, source_target_pairs={{0,7},{1,231},{2,39},{3,199},{4,71},{5,167},{6,103},{7,135},{8,15}... | collective-permute-start | bytes 36872 | tf_op jit(solution)/shard_map/ppermute | solution.py:304

commit v5 on v4

--- a/solution.py
+++ b/solution.py
@@ -229,7 +229,7 @@
         rows = all_ref[source, 0:8, :]
         total = total + rows
         amp_ref[pl.ds(own + folded(source), 1), :] = rows[3:4, C : 2 * C]
-        amp_ref[pl.ds(8 - own + folded(source), 1), :] = rows[4:5, C : 2 * C]
+        amp_ref[pl.ds(8 - own + folded(7 - source ^ 1), 1), :] = rows[4:5, C : 2 * C]
     for step in range(3):
         embed_ref[3 * step : 3 * step + 1, :] = total[step : step + 1, 0:C]
         embed_ref[3 * step + 1 : 3 * step + 2, :] = total[step : step + 1, C : 2 * C]
@@ -273,10 +273,11 @@
 def local(spins, embed_w, block_w, readout, amp_cot):
     own = jnp.broadcast_to(spins, (16, 1, LY))
     fields = lax.all_to_all(own, ("yh", "yl", "core"), 0, 0, tiled=True).reshape(ROWS, LY)
+    fields = pltpu.with_memory_space_constraint(fields, pltpu.VMEM)
     wide = (192, SITES)
     payload = pl.pallas_call(
         main_kernel,
-        out_shape=jax.ShapeDtypeStruct((32 * CHUNK, LY), F32),
+        out_shape=pltpu.VMEM((32 * CHUNK, LY), F32),
         in_specs=vmem(2) + [pl.BlockSpec(memory_space=pl.ANY)] + vmem(2),
         out_specs=pl.BlockSpec(memory_space=pltpu.VMEM),
         scratch_shapes=[
@@ -302,7 +303,7 @@
     parts = lax.all_to_all(payload.reshape(32, CHUNK, LY), ("z", "x"), 0, 0, tiled=True)
     own_sum = jnp.sum(parts, axis=0)
     turned = lax.ppermute(own_sum, ("yh", "z", "x", "yl", "core"), turn_pairs())
-    other = lax.ppermute(own_sum, "yh", [(0, 1), (1, 0)])
+    other = lax.ppermute(own_sum, ("yh", "yl"), [(y, 7 - y) for y in range(8)])
     row = lax.broadcasted_iota(jnp.int32, (CHUNK, LY), 0)
     is_right = lax.broadcasted_iota(jnp.int32, (CHUNK, LY), 1) >= C
     small = jnp.where(is_right & (row == 3), own_sum, jnp.where(is_right & (row == 4), other, own_sum + other))
@@ -310,6 +311,7 @@
     gathered = lax.all_to_all(
         jnp.broadcast_to(mixed, (8, CHUNK, LY)), ("yl", "core"), 0, 0, tiled=True
     )
+    gathered = pltpu.with_memory_space_constraint(gathered, pltpu.VMEM)
     log_amp, block_grad, embed_grad = pl.pallas_call(
         final_kernel,
         out_shape=(

time: 75 us -> 72 us (0.960)
  blocking collectives: 31.9 us -> 29.4 us
  waiting for transfers between devices: 17.3 us -> 19.1 us
  starting transfers between devices: 17.4 us -> 16.1 us
  Pallas kernels: 6.47 us -> 5.58 us
    ppermute x1, waiting for transfers between devices: 1 us -> 3.81 us  [local(): turned = lax.ppermute(own_sum, ('yh', 'z', 'x', 'yl', 'core'), turn_pairs())]
    all_to_all x1, blocking collectives: 14.9 us -> 13.1 us  [local(): lax.all_to_all(jnp.broadcast_to(mixed, (8, CHUNK, LY)), ('yl', 'core'), 0...]
    ppermute x1, starting transfers between devices: 3.7 us -> 1.92 us  [local(): turned = lax.ppermute(own_sum, ('yh', 'z', 'x', 'yl', 'core'), turn_pairs())]
    ppermute x1, waiting for transfers between devices: 2.52 us -> 1.52 us  [local(): other = lax.ppermute(own_sum, ('yh', 'yl'), [(y, 7 - y) for y in range(8)])]
    pallas_call x1, Pallas kernels: 1.69 us -> 0.8 us  [local(): pl.pallas_call(final_kernel, out_shape=(jax.ShapeDtypeStruct((16, C), F32...]
where the time goes in v5:
time: 72 us; the launch traced here: 71.6 us
  blocking collectives  29.4 us (41%)
  waiting for transfers between devices  19.1 us (27%)
  starting transfers between devices  16.1 us (22%)
  Pallas kernels  5.58 us (8%)
    all_to_all x1, blocking collectives, local(): lax.all_to_all(own, ('yh', 'yl', 'core'), 0, 0, tiled=True)  16.3 us
    all_to_all x1, waiting for transfers between devices, local(): lax.all_to_all(payload.reshape(32, CHUNK, LY), ('z', 'x'), 0, 0, tiled=True)  13.8 us
    all_to_all x1, blocking collectives, local(): lax.all_to_all(jnp.broadcast_to(mixed, (8, CHUNK, LY)), ('yl', 'core'), 0...  13.1 us
    all_to_all x1, starting transfers between devices, local(): lax.all_to_all(payload.reshape(32, CHUNK, LY), ('z', 'x'), 0, 0, tiled=True)  12 us
    pallas_call x1, Pallas kernels, local(): pl.pallas_call(main_kernel, out_shape=pltpu.VMEM((32 * CHUNK, LY), F32),...  4.78 us
    ppermute x1, waiting for transfers between devices, local(): turned = lax.ppermute(own_sum, ('yh', 'z', 'x', 'yl', 'core'), turn_pairs())  3.81 us
    ppermute x1, starting transfers between devices, local(): other = lax.ppermute(own_sum, ('yh', 'yl'), [(y, 7 - y) for y in range(8)])  2.18 us
    ppermute x1, starting transfers between devices, local(): turned = lax.ppermute(own_sum, ('yh', 'z', 'x', 'yl', 'core'), turn_pairs())  1.92 us
  transfers between devices with their start and end apart: 3, of which 3 were waited for; matrix products, arithmetic and copies ran while one was open for 0% of the time, Pallas kernels for 0%

profile of v5, /device:TPU:1, one launch (start us, length us, event | category | flops | bytes accessed | tf_op | source)
XLA Modules:
  0.0 71.6 jit_solution(14814741451600931920)
XLA Ops:
  0.6 0.7 broadcast_in_dim.11
  1.3 16.3 %all_to_all.15 = s32[16,1,128]{2,1,0:T(1,128)S(1)} all-to-all(s32[16,1,128]{2,1,0:T(1,128)S(1)} %broadcast_in_dim.11), channel_id=1, replica_groups=mesh['yh'=2,'z'=8,'x'=4,'yl'=4,'core'=2] {'yh','yl','core'}, dimensions={0} | all-to-all | bytes 16384 | tf_op jit(solution)/shard_map/all_to_all | solution.py:275
  17.6 4.8 %states.1 = f32[768,128]{1,0:T(8,128)} custom-call(s32[16,128]{1,0:T(8,128)S(1)} %bitcast.5, bf16[9,64]{1,0:T(8,128)(2,1)} %bitcast.6, bf16[16,1,2,64,576]{4,3,2,1,0:T(8,128)(2,1)} %weight_hbm.1, bf16[16,64]{1,0:T(8,128)(2,1)} %readout_ref.1, f32[16,64]{1,0:T(8,128)} %cot_ref.1), custom_call_target="tpu_custom_call" | custom-call | tf_op jit(solution)/shard_map/states/pallas_call | solution.py:278
  22.4 12.0 %all-to-all-start.1 = ((f32[32,24,128]{2,1,0:T(8,128)}), f32[32,24,128]{2,1,0:T(8,128)S(1)}, u32[]{:S(2)}, u32[]{:S(2)}) async-start(f32[32,24,128]{2,1,0:T(8,128)} %bitcast.3), calls=%async_computation.1 | async-start | bytes 786432 | tf_op jit(solution)/shard_map/all_to_all | solution.py:303
  34.4 13.8 %all-to-all-done.1 = f32[32,24,128]{2,1,0:T(8,128)S(1)} async-done(((f32[32,24,128]{2,1,0:T(8,128)}), f32[32,24,128]{2,1,0:T(8,128)S(1)}, u32[]{:S(2)}, u32[]{:S(2)}) %all-to-all-start.1) | async-done | bytes 393248 | tf_op jit(solution)/shard_map/all_to_all | solution.py:303
  48.2 2.2 %collective-permute-start = (f32[24,128]{1,0:T(8,128)S(1)}, f32[24,128]{1,0:T(8,128)S(1)}, u32[]{:S(2)}, u32[]{:S(2)}) collective-permute-start(f32[24,128]{1,0:T(8,128)S(1)} %reduce_sum.9), channel_id=1, source_target_pairs={{0,262},{2,260},{4,258},{6,256},{256,6},{258,4},{260,2},{262,0},{1... | collective-permute-start | bytes 36872 | tf_op jit(solution)/shard_map/ppermute | solution.py:306
  50.4 1.9 %collective-permute-start.1 = (f32[24,128]{1,0:T(8,128)S(1)}, f32[24,128]{1,0:T(8,128)S(1)}, u32[]{:S(2)}, u32[]{:S(2)}) collective-permute-start(f32[24,128]{1,0:T(8,128)S(1)} %reduce_sum.9), channel_id=1, source_target_pairs={{0,7},{1,231},{2,39},{3,199},{4,71},{5,167},{6,103},{7,135},{8,15}... | collective-permute-start | bytes 36872 | tf_op jit(solution)/shard_map/ppermute | solution.py:305
  52.4 1.5 %collective-permute-done = f32[24,128]{1,0:T(8,128)S(1)} collective-permute-done((f32[24,128]{1,0:T(8,128)S(1)}, f32[24,128]{1,0:T(8,128)S(1)}, u32[]{:S(2)}, u32[]{:S(2)}) %collective-permute-start) | collective-permute-done | bytes 12320 | tf_op jit(solution)/shard_map/ppermute | solution.py:306
  53.9 3.8 %collective-permute-done.1 = f32[24,128]{1,0:T(8,128)S(1)} collective-permute-done((f32[24,128]{1,0:T(8,128)S(1)}, f32[24,128]{1,0:T(8,128)S(1)}, u32[]{:S(2)}, u32[]{:S(2)}) %collective-permute-start.1) | collective-permute-done | bytes 12320 | tf_op jit(solution)/shard_map/ppermute | solution.py:305
  57.7 0.1 fusion.1
  57.8 13.1 %all_to_all.16.all_ref = f32[8,24,128]{2,1,0:T(8,128)S(1)} all-to-all(f32[8,24,128]{2,1,0:T(8,128)S(1)} %broadcast_in_dim.12), channel_id=1, replica_groups=mesh['yh'=2,'z'=8,'x'=4,'yl'=4,'core'=2] {'yl','core'}, dimensions={0} | all-to-all | bytes 196608 | tf_op jit(solution)/shard_map/all_to_all | solution.py:311
  70.8 0.8 %outputs.1 = (f32[16,64]{1,0:T(8,128)}, f32[16,1,2,576]{3,2,1,0:T(2,128)}, f32[9,64]{1,0:T(8,128)}) custom-call(f32[8,24,128]{2,1,0:T(8,128)S(1)} %all_to_all.16.all_ref), custom_call_target="tpu_custom_call" | custom-call | tf_op jit(solution)/shard_map/outputs/pallas_call | solution.py:315
  (5 shorter events, 0.1 us)
Async XLA Ops:
  22.4 25.8 %all-to-all-start.1 = ((f32[32,24,128]{2,1,0:T(8,128)}), f32[32,24,128]{2,1,0:T(8,128)S(1)}, u32[]{:S(2)}, u32[]{:S(2)}) async-start(f32[32,24,128]{2,1,0:T(8,128)} %bitcast.3), calls=%async_computation.1 | async-start | bytes 786432 | tf_op jit(solution)/shard_map/all_to_all | solution.py:303
  48.2 5.7 %collective-permute-start = (f32[24,128]{1,0:T(8,128)S(1)}, f32[24,128]{1,0:T(8,128)S(1)}, u32[]{:S(2)}, u32[]{:S(2)}) collective-permute-start(f32[24,128]{1,0:T(8,128)S(1)} %reduce_sum.9), channel_id=1, source_target_pairs={{0,262},{2,260},{4,258},{6,256},{256,6},{258,4},{260,2},{262,0},{1... | collective-permute-start | bytes 36872 | tf_op jit(solution)/shard_map/ppermute | solution.py:306
  50.4 7.3 %collective-permute-start.1 = (f32[24,128]{1,0:T(8,128)S(1)}, f32[24,128]{1,0:T(8,128)S(1)}, u32[]{:S(2)}, u32[]{:S(2)}) collective-permute-start(f32[24,128]{1,0:T(8,128)S(1)} %reduce_sum.9), channel_id=1, source_target_pairs={{0,7},{1,231},{2,39},{3,199},{4,71},{5,167},{6,103},{7,135},{8,15}... | collective-permute-start | bytes 36872 | tf_op jit(solution)/shard_map/ppermute | solution.py:305

commit v6 on v5

--- a/solution.py
+++ b/solution.py
@@ -69,16 +69,54 @@
     return 1.0 / (1.0 + jnp.exp(-v))
 
 
-def main_kernel(
+def own_state():
+    along = lax.axis_index("yl")
+    return lax.axis_index("yh") * 8 + jnp.where(lax.axis_index("core") == 0, along, 7 - along)
+
+
+def own_walker():
+    return lax.axis_index("z") * 4 + lax.axis_index("x")
+
+
+def weights_kernel(
+    embed_ref, weight_hbm, readout_ref, cot_ref, wf_ref, wt_ref, taps_ref, column_ref, w_ref, sem
+):
+    state = own_state()
+    copy = pltpu.make_async_copy(weight_hbm.at[state, 0], w_ref, sem)
+    copy.start()
+    embed = embed_ref[...].astype(F32)
+    nothing = jnp.zeros((5, C), F32)
+    rows = []
+    for step in range(3):
+        rows += [embed[3 * k + step : 3 * k + step + 1] for k in range(3)] + [nothing]
+    taps_ref[...] = jnp.transpose(jnp.concatenate(rows, axis=0)).astype(BF16)
+
+    pick = lax.broadcasted_iota(jnp.int32, (16, C), 0) == state
+    readout = jnp.where(pick, readout_ref[...].astype(F32), 0.0)
+    column = jnp.sum(jnp.transpose(readout), axis=1, keepdims=True)
+    cot_row = jnp.sum(jnp.where(pick, cot_ref[...], 0.0), axis=0, keepdims=True)
+    walker_lane = lax.broadcasted_iota(jnp.int32, (1, C), 1)
+    columns = [column]
+    for k in range(2):
+        mine = jnp.where(walker_lane == own_walker() + 32 * k, cot_row, 0.0)
+        columns.append(jnp.sum(mine, axis=1, keepdims=True) * SCALE * column)
+    for k in range(3):
+        column_ref[k] = jnp.broadcast_to(columns[k], (C, LY))
+
+    copy.wait()
+    for block in range(2):
+        for step in range(3):
+            wf_ref[block, step * C : (step + 1) * C, :] = w_ref[block][:, 192 * step : 192 * step + 192]
+        wt_ref[block] = jnp.transpose(wf_ref[block].astype(F32)).astype(BF16)
+
+
+def states_kernel(
     spin_ref,
-    embed_ref,
-    weight_hbm,
-    readout_ref,
-    cot_ref,
-    out_ref,
-    w_ref,
     wf_ref,
     wt_ref,
+    taps_ref,
+    column_ref,
+    out_ref,
     pad_ref,
     patch_ref,
     h_ref,
@@ -91,13 +129,8 @@
     ya_ref,
     yb_ref,
     parts_ref,
-    sem,
 ):
-    along = lax.axis_index("yl")
-    state = lax.axis_index("yh") * 8 + jnp.where(lax.axis_index("core") == 0, along, 7 - along)
-    first_walker = lax.axis_index("z") * 4 + lax.axis_index("x")
-    copy = pltpu.make_async_copy(weight_hbm.at[state, 0], w_ref, sem)
-    copy.start()
+    first_walker = own_walker()
     halves = [range(half * LX, half * LX + LX) for half in range(2)]
 
     spin = spin_ref[...].astype(F32)
@@ -106,12 +139,7 @@
         for step, value in enumerate((pltpu.roll(turned, 1, 1), turned, pltpu.roll(turned, LY - 1, 1))):
             pad_ref[step, half * 16 : half * 16 + 8] = value
             pad_ref[step, half * 16 + 8 : half * 16 + 16] = value
-    embed = embed_ref[...].astype(F32)
-    nothing = jnp.zeros((5, C), F32)
-    rows = []
-    for step in range(3):
-        rows += [embed[3 * k + step : 3 * k + step + 1] for k in range(3)] + [nothing]
-    embed24 = jnp.transpose(jnp.concatenate(rows, axis=0)).astype(BF16)
+    embed24 = taps_ref[...]
     for half in range(2):
         for row in halves[half]:
             first = half * 16 + row % LX
@@ -125,23 +153,6 @@
             h_ref[:, lanes(row)] = value.astype(F32)
             store_shifted(hc_ref, row, value)
 
-    pick = lax.broadcasted_iota(jnp.int32, (16, C), 0) == state
-    readout = jnp.where(pick, readout_ref[...].astype(F32), 0.0)
-    column = jnp.sum(jnp.transpose(readout), axis=1, keepdims=True)
-    cot_row = jnp.sum(jnp.where(pick, cot_ref[...], 0.0), axis=0, keepdims=True)
-    walker_lane = lax.broadcasted_iota(jnp.int32, (1, C), 1)
-    cots = [
-        jnp.sum(jnp.where(walker_lane == first_walker + 32 * k, cot_row, 0.0), axis=1, keepdims=True)
-        * SCALE
-        for k in range(2)
-    ]
-
-    copy.wait()
-    for block in range(2):
-        for step in range(3):
-            wf_ref[block, step * C : (step + 1) * C, :] = w_ref[block][:, 192 * step : 192 * step + 192]
-        wt_ref[block] = jnp.transpose(wf_ref[block].astype(F32)).astype(BF16)
-
     def first_act(half):
         for row in halves[half]:
             z = gather_rows(ya_ref, row)
@@ -150,7 +161,7 @@
             store_shifted(gc_ref, row, (z * sig).astype(BF16))
 
     def second_act(half):
-        weight = cots[half] * column
+        weight = column_ref[1 + half]
         total = jnp.zeros((C, LY), F32)
         for row in halves[half]:
             u = h_ref[:, lanes(row)] + gather_rows(yb_ref, row)
@@ -160,7 +171,7 @@
             stream_ref[:, lanes(row)] = d
             store_spread(d2_ref, row, d.astype(BF16))
         return (
-            jnp.sum(jnp.sum(total * column, axis=0, keepdims=True), axis=1, keepdims=True) * SCALE
+            jnp.sum(jnp.sum(total * column_ref[0], axis=0, keepdims=True), axis=1, keepdims=True) * SCALE
         )
 
     def first_back(half):
@@ -275,15 +286,26 @@
     fields = lax.all_to_all(own, ("yh", "yl", "core"), 0, 0, tiled=True).reshape(ROWS, LY)
     fields = pltpu.with_memory_space_constraint(fields, pltpu.VMEM)
     wide = (192, SITES)
+    weights = pl.pallas_call(
+        weights_kernel,
+        out_shape=(
+            pltpu.VMEM((2, 192, 192), BF16),
+            pltpu.VMEM((2, 192, 192), BF16),
+            pltpu.VMEM((C, 24), BF16),
+            pltpu.VMEM((3, C, LY), F32),
+        ),
+        in_specs=vmem(1) + [pl.BlockSpec(memory_space=pl.ANY)] + vmem(2),
+        out_specs=tuple(vmem(4)),
+        scratch_shapes=[pltpu.VMEM((2, C, 576), BF16), pltpu.SemaphoreType.DMA],
+        name="weights",
+    )(embed_w.T, block_w, readout, amp_cot)
+    weights = [pltpu.with_memory_space_constraint(value, pltpu.VMEM) for value in weights]
     payload = pl.pallas_call(
-        main_kernel,
+        states_kernel,
         out_shape=pltpu.VMEM((32 * CHUNK, LY), F32),
-        in_specs=vmem(2) + [pl.BlockSpec(memory_space=pl.ANY)] + vmem(2),
+        in_specs=vmem(5),
         out_specs=pl.BlockSpec(memory_space=pltpu.VMEM),
         scratch_shapes=[
-            pltpu.VMEM((2, C, 576), BF16),
-            pltpu.VMEM((2, 192, 192), BF16),
-            pltpu.VMEM((2, 192, 192), BF16),
             pltpu.VMEM((3, 32, LY), F32),
             pltpu.VMEM((24, SITES), BF16),
             pltpu.VMEM((C, SITES), F32),
@@ -296,16 +318,16 @@
             pltpu.VMEM(wide, F32),
             pltpu.VMEM(wide, F32),
             pltpu.VMEM((2 * C, SITES), BF16),
-            pltpu.SemaphoreType.DMA,
         ],
         name="states",
-    )(fields, embed_w.T, block_w, readout, amp_cot)
+    )(fields, *weights)
     parts = lax.all_to_all(payload.reshape(32, CHUNK, LY), ("z", "x"), 0, 0, tiled=True)
     own_sum = jnp.sum(parts, axis=0)
     turned = lax.ppermute(own_sum, ("yh", "z", "x", "yl", "core"), turn_pairs())
     other = lax.ppermute(own_sum, ("yh", "yl"), [(y, 7 - y) for y in range(8)])
     row = lax.broadcasted_iota(jnp.int32, (CHUNK, LY), 0)
-    is_right = lax.broadcasted_iota(jnp.int32, (CHUNK, LY), 1) >= C
+    own_sum, row, column = lax.optimization_barrier((own_sum, row, lax.broadcasted_iota(jnp.int32, (CHUNK, LY), 1)))
+    is_right = column >= C
     small = jnp.where(is_right & (row == 3), own_sum, jnp.where(is_right & (row == 4), other, own_sum + other))
     mixed = jnp.where(row < HEAD, small, turned)
     gathered = lax.all_to_all(

time: 72 us -> 70.2 us (0.975)
  waiting for transfers between devices: 19.1 us -> 10.4 us
  blocking collectives: 29.4 us -> 38 us
  starting transfers between devices: 16.1 us -> 14.2 us
    all_to_all x1, waiting for transfers between devices: 13.8 us -> 5.07 us  [local(): lax.all_to_all(own, ('yh', 'yl', 'core'), 0, 0, tiled=True)]
    all_to_all x1, blocking collectives: 16.3 us -> 24.9 us  [local(): lax.all_to_all(payload.reshape(32, CHUNK, LY), ('z', 'x'), 0, 0, tiled=True)]
    all_to_all x1, starting transfers between devices: 12 us -> 10.1 us  [local(): lax.all_to_all(own, ('yh', 'yl', 'core'), 0, 0, tiled=True)]
    pallas_call x1 -> x2, Pallas kernels: 4.78 us -> 4.45 us  [the longest x1 2.54 us: local(): pl.pallas_call(states_kernel, out_shape=pltpu.VMEM((32 * CHUNK, LY), F32)...]
  transfers between devices with their start and end apart: 3 -> 3, of which waited for: 3 -> 3; matrix products, arithmetic and copies ran while one was open for 0% -> 0% of each run, Pallas kernels for 0% -> 3%
where the time goes in v6:
time: 70.2 us; the launch traced here: 69.9 us
  blocking collectives  38 us (54%)
  starting transfers between devices  14.2 us (20%)
  waiting for transfers between devices  10.4 us (15%)
  Pallas kernels  5.25 us (7%)
  local copies, waits for them, and re-layouts  1.28 us (2%)
    all_to_all x1, blocking collectives, local(): lax.all_to_all(payload.reshape(32, CHUNK, LY), ('z', 'x'), 0, 0, tiled=True)  24.9 us
    all_to_all x1, blocking collectives, local(): lax.all_to_all(jnp.broadcast_to(mixed, (8, CHUNK, LY)), ('yl', 'core'), 0...  13.1 us
    all_to_all x1, starting transfers between devices, local(): lax.all_to_all(own, ('yh', 'yl', 'core'), 0, 0, tiled=True)  10.1 us
    all_to_all x1, waiting for transfers between devices, local(): lax.all_to_all(own, ('yh', 'yl', 'core'), 0, 0, tiled=True)  5.07 us
    ppermute x1, waiting for transfers between devices, local(): turned = lax.ppermute(own_sum, ('yh', 'z', 'x', 'yl', 'core'), turn_pairs())  3.8 us
    pallas_call x1, Pallas kernels, local(): pl.pallas_call(states_kernel, out_shape=pltpu.VMEM((32 * CHUNK, LY), F32)...  2.54 us
    ppermute x1, starting transfers between devices, local(): other = lax.ppermute(own_sum, ('yh', 'yl'), [(y, 7 - y) for y in range(8)])  2.18 us
    ppermute x1, starting transfers between devices, local(): turned = lax.ppermute(own_sum, ('yh', 'z', 'x', 'yl', 'core'), turn_pairs())  1.92 us
  transfers between devices with their start and end apart: 3, of which 3 were waited for; matrix products, arithmetic and copies ran while one was open for 0% of the time, Pallas kernels for 3%

profile of v6, /device:TPU:1, one launch (start us, length us, event | category | flops | bytes accessed | tf_op | source)
XLA Modules:
  0.0 69.9 jit_solution(18341346912701755550)
XLA Ops:
  0.6 1.3 %broadcast_in_dim.11 = s32[16,1,128]{2,1,0:T(1,128)} broadcast(s32[128]{0:T(128)} %bitcast.8), dimensions={2} | broadcast | bytes 8704 | tf_op jit(solution)/shard_map/broadcast_in_dim | solution.py:285
  1.9 10.1 %all-to-all-start = ((s32[16,1,128]{2,1,0:T(1,128)}), s32[16,1,128]{2,1,0:T(1,128)S(1)}, u32[]{:S(2)}, u32[]{:S(2)}) async-start(s32[16,1,128]{2,1,0:T(1,128)} %broadcast_in_dim.11), calls=%async_computation | async-start | bytes 16384 | tf_op jit(solution)/shard_map/all_to_all | solution.py:286
  12.0 1.9 %weights.1 = (bf16[2,192,192]{2,1,0:T(8,128)(2,1)S(1)}, bf16[2,192,192]{2,1,0:T(8,128)(2,1)S(1)}, bf16[64,24]{1,0:T(8,128)(2,1)S(1)}, f32[3,64,128]{2,1,0:T(8,128)S(1)}) custom-call(bf16[9,64]{1,0:T(8,128)(2,1)} %bitcast.7, bf16[16,1,2,64,576]{4,3,2,1,0:T(8,128)(2,1)} %weight_hbm.1, bf16[16,64]{1,0:T(8,128)(2,1)} %readout_ref.1, f32[16,64]{1,0:T(8,128)} %cot_ref.1), custom_call_target="tpu_custom_call" | custom-call | tf_op jit(solution)/shard_map/weights/pallas_call | solution.py:289
  13.9 5.1 %all-to-all-done = s32[16,1,128]{2,1,0:T(1,128)S(1)} async-done(((s32[16,1,128]{2,1,0:T(1,128)}), s32[16,1,128]{2,1,0:T(1,128)S(1)}, u32[]{:S(2)}, u32[]{:S(2)}) %all-to-all-start) | async-done | bytes 8224 | tf_op jit(solution)/shard_map/all_to_all | solution.py:286
  19.0 2.5 %states.1 = f32[768,128]{1,0:T(8,128)S(1)} custom-call(s32[16,128]{1,0:T(8,128)S(1)} %bitcast.6, bf16[2,192,192]{2,1,0:T(8,128)(2,1)S(1)} %get-tuple-element.13.wf_ref, bf16[2,192,192]{2,1,0:T(8,128)(2,1)S(1)} %get-tuple-element.14.wt_ref, bf16[64,24]{1,0:T(8,128)(2,1)S(1)} %get-tuple-element.15.taps_ref, f32[3,64,128]{2,1,0:T(8,128)S(1)} %get-tuple-element.16.column_ref), custom_call_target="tpu_custom_call" | custom-call | tf_op jit(solution)/shard_map/states/pallas_call | solution.py:303
  21.6 24.9 %all_to_all.15 = f32[32,24,128]{2,1,0:T(8,128)S(1)} all-to-all(f32[32,24,128]{2,1,0:T(8,128)S(1)} %bitcast.5), channel_id=1, replica_groups=mesh['yh'=2,'z'=8,'x'=4,'yl'=4,'core'=2] {'z','x'}, dimensions={0} | all-to-all | bytes 786432 | tf_op jit(solution)/shard_map/all_to_all | solution.py:324
  46.5 2.2 %collective-permute-start = (f32[24,128]{1,0:T(8,128)S(1)}, f32[24,128]{1,0:T(8,128)S(1)}, u32[]{:S(2)}, u32[]{:S(2)}) collective-permute-start(f32[24,128]{1,0:T(8,128)S(1)} %reduce_sum.9), channel_id=1, source_target_pairs={{0,262},{2,260},{4,258},{6,256},{256,6},{258,4},{260,2},{262,0},{1... | collective-permute-start | bytes 36872 | tf_op jit(solution)/shard_map/ppermute | solution.py:327
  48.7 1.9 %collective-permute-start.1 = (f32[24,128]{1,0:T(8,128)S(1)}, f32[24,128]{1,0:T(8,128)S(1)}, u32[]{:S(2)}, u32[]{:S(2)}) collective-permute-start(f32[24,128]{1,0:T(8,128)S(1)} %reduce_sum.9), channel_id=1, source_target_pairs={{0,7},{1,231},{2,39},{3,199},{4,71},{5,167},{6,103},{7,135},{8,15}... | collective-permute-start | bytes 36872 | tf_op jit(solution)/shard_map/ppermute | solution.py:326
  50.6 1.5 %collective-permute-done = f32[24,128]{1,0:T(8,128)S(1)} collective-permute-done((f32[24,128]{1,0:T(8,128)S(1)}, f32[24,128]{1,0:T(8,128)S(1)}, u32[]{:S(2)}, u32[]{:S(2)}) %collective-permute-start) | collective-permute-done | bytes 12320 | tf_op jit(solution)/shard_map/ppermute | solution.py:327
  52.2 3.8 %collective-permute-done.1 = f32[24,128]{1,0:T(8,128)S(1)} collective-permute-done((f32[24,128]{1,0:T(8,128)S(1)}, f32[24,128]{1,0:T(8,128)S(1)}, u32[]{:S(2)}, u32[]{:S(2)}) %collective-permute-start.1) | collective-permute-done | bytes 12320 | tf_op jit(solution)/shard_map/ppermute | solution.py:326
  56.0 13.1 %all_to_all.16.all_ref = f32[8,24,128]{2,1,0:T(8,128)S(1)} all-to-all(f32[8,24,128]{2,1,0:T(8,128)S(1)} %broadcast_in_dim.12), channel_id=1, replica_groups=mesh['yh'=2,'z'=8,'x'=4,'yl'=4,'core'=2] {'yl','core'}, dimensions={0} | all-to-all | bytes 196608 | tf_op jit(solution)/shard_map/all_to_all | solution.py:333
  69.1 0.8 %outputs.1 = (f32[16,64]{1,0:T(8,128)}, f32[16,1,2,576]{3,2,1,0:T(2,128)}, f32[9,64]{1,0:T(8,128)}) custom-call(f32[8,24,128]{2,1,0:T(8,128)S(1)} %all_to_all.16.all_ref), custom_call_target="tpu_custom_call" | custom-call | tf_op jit(solution)/shard_map/outputs/pallas_call | solution.py:337
  (5 shorter events, 0.1 us)
Async XLA Ops:
  1.9 17.1 %all-to-all-start = ((s32[16,1,128]{2,1,0:T(1,128)}), s32[16,1,128]{2,1,0:T(1,128)S(1)}, u32[]{:S(2)}, u32[]{:S(2)}) async-start(s32[16,1,128]{2,1,0:T(1,128)} %broadcast_in_dim.11), calls=%async_computation | async-start | bytes 16384 | tf_op jit(solution)/shard_map/all_to_all | solution.py:286
  46.5 5.7 %collective-permute-start = (f32[24,128]{1,0:T(8,128)S(1)}, f32[24,128]{1,0:T(8,128)S(1)}, u32[]{:S(2)}, u32[]{:S(2)}) collective-permute-start(f32[24,128]{1,0:T(8,128)S(1)} %reduce_sum.9), channel_id=1, source_target_pairs={{0,262},{2,260},{4,258},{6,256},{256,6},{258,4},{260,2},{262,0},{1... | collective-permute-start | bytes 36872 | tf_op jit(solution)/shard_map/ppermute | solution.py:327
  48.7 7.3 %collective-permute-start.1 = (f32[24,128]{1,0:T(8,128)S(1)}, f32[24,128]{1,0:T(8,128)S(1)}, u32[]{:S(2)}, u32[]{:S(2)}) collective-permute-start(f32[24,128]{1,0:T(8,128)S(1)} %reduce_sum.9), channel_id=1, source_target_pairs={{0,7},{1,231},{2,39},{3,199},{4,71},{5,167},{6,103},{7,135},{8,15}... | collective-permute-start | bytes 36872 | tf_op jit(solution)/shard_map/ppermute | solution.py:326

commit v7 on v6

--- a/solution.py
+++ b/solution.py
@@ -69,9 +69,11 @@
     return 1.0 / (1.0 + jnp.exp(-v))
 
 
-def own_state():
+def state_of(which):
     along = lax.axis_index("yl")
-    return lax.axis_index("yh") * 8 + jnp.where(lax.axis_index("core") == 0, along, 7 - along)
+    high = lax.axis_index("yh")
+    high = high if which == 0 else 1 - high
+    return high * 8 + jnp.where(lax.axis_index("core") == 0, along, 7 - along)
 
 
 def own_walker():
@@ -81,9 +83,13 @@
 def weights_kernel(
     embed_ref, weight_hbm, readout_ref, cot_ref, wf_ref, wt_ref, taps_ref, column_ref, w_ref, sem
 ):
-    state = own_state()
-    copy = pltpu.make_async_copy(weight_hbm.at[state, 0], w_ref, sem)
-    copy.start()
+    copies = []
+    for which in range(2):
+        copy = pltpu.make_async_copy(
+            weight_hbm.at[state_of(which), 0], w_ref.at[which], sem.at[which]
+        )
+        copy.start()
+        copies.append(copy)
     embed = embed_ref[...].astype(F32)
     nothing = jnp.zeros((5, C), F32)
     rows = []
@@ -91,23 +97,27 @@
         rows += [embed[3 * k + step : 3 * k + step + 1] for k in range(3)] + [nothing]
     taps_ref[...] = jnp.transpose(jnp.concatenate(rows, axis=0)).astype(BF16)
 
-    pick = lax.broadcasted_iota(jnp.int32, (16, C), 0) == state
-    readout = jnp.where(pick, readout_ref[...].astype(F32), 0.0)
-    column = jnp.sum(jnp.transpose(readout), axis=1, keepdims=True)
-    cot_row = jnp.sum(jnp.where(pick, cot_ref[...], 0.0), axis=0, keepdims=True)
     walker_lane = lax.broadcasted_iota(jnp.int32, (1, C), 1)
-    columns = [column]
-    for k in range(2):
-        mine = jnp.where(walker_lane == own_walker() + 32 * k, cot_row, 0.0)
-        columns.append(jnp.sum(mine, axis=1, keepdims=True) * SCALE * column)
-    for k in range(3):
-        column_ref[k] = jnp.broadcast_to(columns[k], (C, LY))
-
-    copy.wait()
-    for block in range(2):
-        for step in range(3):
-            wf_ref[block, step * C : (step + 1) * C, :] = w_ref[block][:, 192 * step : 192 * step + 192]
-        wt_ref[block] = jnp.transpose(wf_ref[block].astype(F32)).astype(BF16)
+    for which in range(2):
+        pick = lax.broadcasted_iota(jnp.int32, (16, C), 0) == state_of(which)
+        readout = jnp.where(pick, readout_ref[...].astype(F32), 0.0)
+        column = jnp.sum(jnp.transpose(readout), axis=1, keepdims=True)
+        cot_row = jnp.sum(jnp.where(pick, cot_ref[...], 0.0), axis=0, keepdims=True)
+        columns = [column]
+        for k in range(2):
+            mine = jnp.where(walker_lane == own_walker() + 32 * k, cot_row, 0.0)
+            columns.append(jnp.sum(mine, axis=1, keepdims=True) * SCALE * column)
+        for k in range(3):
+            column_ref[which, k] = jnp.broadcast_to(columns[k], (C, LY))
+
+    for which in range(2):
+        copies[which].wait()
+        for block in range(2):
+            for step in range(3):
+                wf_ref[which, block, step * C : (step + 1) * C, :] = w_ref[which, block][
+                    :, 192 * step : 192 * step + 192
+                ]
+            wt_ref[which, block] = jnp.transpose(wf_ref[which, block].astype(F32)).astype(BF16)
 
 
 def states_kernel(
@@ -153,56 +163,68 @@
             h_ref[:, lanes(row)] = value.astype(F32)
             store_shifted(hc_ref, row, value)
 
-    def first_act(half):
-        for row in halves[half]:
-            z = gather_rows(ya_ref, row)
+    def first_act(which, half):
+        for row in halves[half]:
+            z = gather_rows(ya_ref.at[which], row)
             sig = sigmoid(z)
-            slope_ref[:, lanes(row)] = sig * (1.0 + z * (1.0 - sig))
-            store_shifted(gc_ref, row, (z * sig).astype(BF16))
-
-    def second_act(half):
-        weight = column_ref[1 + half]
+            slope_ref[which, :, lanes(row)] = sig * (1.0 + z * (1.0 - sig))
+            store_shifted(gc_ref.at[which], row, (z * sig).astype(BF16))
+
+    def second_act(which, half):
+        weight = column_ref[which, 1 + half]
         total = jnp.zeros((C, LY), F32)
         for row in halves[half]:
-            u = h_ref[:, lanes(row)] + gather_rows(yb_ref, row)
+            u = h_ref[:, lanes(row)] + gather_rows(yb_ref.at[which], row)
             sig = sigmoid(u)
             total = total + u * sig
             d = weight * (sig * (1.0 + u * (1.0 - sig)))
-            stream_ref[:, lanes(row)] = d
-            store_spread(d2_ref, row, d.astype(BF16))
-        return (
-            jnp.sum(jnp.sum(total * column_ref[0], axis=0, keepdims=True), axis=1, keepdims=True) * SCALE
-        )
-
-    def first_back(half):
-        for row in halves[half]:
-            dz = (gather_cols(ya_ref, row) * slope_ref[:, lanes(row)]).astype(BF16)
-            store_spread(d1_ref, row, dz)
+            stream_ref[which, :, lanes(row)] = d
+            store_spread(d2_ref.at[which], row, d.astype(BF16))
+        total = jnp.sum(total * column_ref[which, 0], axis=0, keepdims=True)
+        return jnp.sum(total, axis=1, keepdims=True) * SCALE
+
+    def first_back(which, half):
+        for row in halves[half]:
+            dz = gather_cols(ya_ref.at[which], row) * slope_ref[which, :, lanes(row)]
+            store_spread(d1_ref.at[which], row, dz.astype(BF16))
 
     def last_back(half):
         for row in halves[half]:
-            dh = stream_ref[:, lanes(row)] + gather_cols(yb_ref, row)
+            sums = [
+                stream_ref[which, :, lanes(row)] + gather_cols(yb_ref.at[which], row)
+                for which in range(2)
+            ]
+            dh = sums[0] + sums[1]
             high = dh.astype(BF16)
             parts_ref[0:C, lanes(row)] = high
             parts_ref[C : 2 * C, lanes(row)] = (dh - high.astype(F32)).astype(BF16)
 
-    matmul(wf_ref[0], hc_ref, ya_ref, 0)
-    matmul(wf_ref[0], hc_ref, ya_ref, 1)
-    first_act(0)
-    matmul(wf_ref[1], gc_ref, yb_ref, 0)
-    first_act(1)
-    matmul(wf_ref[1], gc_ref, yb_ref, 1)
-    amps = [second_act(0)]
-    matmul(wt_ref[1], d2_ref, ya_ref, 0)
-    amps.append(second_act(1))
-    matmul(wt_ref[1], d2_ref, ya_ref, 1)
-    first_back(0)
-    grad_two = dot_nt(d2_ref[...], gc_ref[...])
-    matmul(wt_ref[0], d1_ref, yb_ref, 0)
-    first_back(1)
-    matmul(wt_ref[0], d1_ref, yb_ref, 1)
+    def store_thirds(third, value):
+        for step in range(3):
+            for upper in range(2):
+                place = HEAD + (third * 3 + step) * 2 + upper
+                for quarter in range(4):
+                    base = step * C + quarter * 16 + upper * 8
+                    out_ref[pl.ds(quarter * CHUNK + place, 8, stride=4 * CHUNK), :] = value[
+                        base : base + 8, :
+                    ]
+
+    pairs = [(which, half) for which in range(2) for half in range(2)]
+    for which, half in pairs:
+        matmul(wf_ref[which, 0], hc_ref, ya_ref.at[which], half)
+    for which, half in pairs:
+        first_act(which, half)
+        matmul(wf_ref[which, 1], gc_ref.at[which], yb_ref.at[which], half)
+    amps = {}
+    for which, half in pairs:
+        amps[which, half] = second_act(which, half)
+        matmul(wt_ref[which, 1], d2_ref.at[which], ya_ref.at[which], half)
+    grad_two = dot_nt(d2_ref[0], gc_ref[0])
+    for which, half in pairs:
+        first_back(which, half)
+        matmul(wt_ref[which, 0], d1_ref.at[which], yb_ref.at[which], half)
+    grad_one = dot_nt(d1_ref[0], hc_ref[...])
     last_back(0)
-    grad_one = dot_nt(d1_ref[...], hc_ref[...])
     last_back(1)
     both = dot_nt(parts_ref[...], patch_ref[...])
     taps = jnp.transpose(both[0:C] + both[C : 2 * C])
@@ -212,25 +234,14 @@
     left = jnp.concatenate([taps[0:3], taps[16:19], jnp.zeros((2, C), F32)], axis=0)
     right = jnp.concatenate([taps[8:11], jnp.zeros((5, C), F32)], axis=0)
     small = jnp.concatenate([left, right], axis=1)
-    for k in range(2):
-        here = ((sub == 3) | (sub == 4)) & (lane == C + first_walker + 32 * k)
-        small = jnp.where(here, amps[k], small)
-    thirds = (
-        grad_one[:, 0:LY],
-        grad_two[:, 0:LY],
-        jnp.concatenate([grad_one[:, LY:192], grad_two[:, LY:192]], axis=1),
-    )
+    for which, half in pairs:
+        here = (sub == 3 + which) & (lane == C + first_walker + 32 * half)
+        small = jnp.where(here, amps[which, half], small)
     for chunk in range(32):
         out_ref[chunk * CHUNK : chunk * CHUNK + 8, :] = small
-    for third in range(3):
-        for step in range(3):
-            for upper in range(2):
-                place = HEAD + (third * 3 + step) * 2 + upper
-                for quarter in range(4):
-                    base = step * C + quarter * 16 + upper * 8
-                    out_ref[pl.ds(quarter * CHUNK + place, 8, stride=4 * CHUNK), :] = thirds[third][
-                        base : base + 8, :
-                    ]
+    store_thirds(0, grad_one[:, 0:LY])
+    store_thirds(1, grad_two[:, 0:LY])
+    store_thirds(2, jnp.concatenate([grad_one[:, LY:192], grad_two[:, LY:192]], axis=1))
 
 
 def final_kernel(all_ref, amp_ref, out_ref, embed_ref):
@@ -240,7 +251,7 @@
         rows = all_ref[source, 0:8, :]
         total = total + rows
         amp_ref[pl.ds(own + folded(source), 1), :] = rows[3:4, C : 2 * C]
-        amp_ref[pl.ds(8 - own + folded(7 - source ^ 1), 1), :] = rows[4:5, C : 2 * C]
+        amp_ref[pl.ds(8 - own + folded(source), 1), :] = rows[4:5, C : 2 * C]
     for step in range(3):
         embed_ref[3 * step : 3 * step + 1, :] = total[step : step + 1, 0:C]
         embed_ref[3 * step + 1 : 3 * step + 2, :] = total[step : step + 1, C : 2 * C]
@@ -285,18 +296,18 @@
     own = jnp.broadcast_to(spins, (16, 1, LY))
     fields = lax.all_to_all(own, ("yh", "yl", "core"), 0, 0, tiled=True).reshape(ROWS, LY)
     fields = pltpu.with_memory_space_constraint(fields, pltpu.VMEM)
-    wide = (192, SITES)
+    pair = (2, 192, SITES)
     weights = pl.pallas_call(
         weights_kernel,
         out_shape=(
-            pltpu.VMEM((2, 192, 192), BF16),
-            pltpu.VMEM((2, 192, 192), BF16),
+            pltpu.VMEM((2, 2, 192, 192), BF16),
+            pltpu.VMEM((2, 2, 192, 192), BF16),
             pltpu.VMEM((C, 24), BF16),
-            pltpu.VMEM((3, C, LY), F32),
+            pltpu.VMEM((2, 3, C, LY), F32),
         ),
         in_specs=vmem(1) + [pl.BlockSpec(memory_space=pl.ANY)] + vmem(2),
         out_specs=tuple(vmem(4)),
-        scratch_shapes=[pltpu.VMEM((2, C, 576), BF16), pltpu.SemaphoreType.DMA],
+        scratch_shapes=[pltpu.VMEM((2, 2, C, 576), BF16), pltpu.SemaphoreType.DMA((2,))],
         name="weights",
     )(embed_w.T, block_w, readout, amp_cot)
     weights = [pltpu.with_memory_space_constraint(value, pltpu.VMEM) for value in weights]
@@ -309,14 +320,14 @@
             pltpu.VMEM((3, 32, LY), F32),
             pltpu.VMEM((24, SITES), BF16),
             pltpu.VMEM((C, SITES), F32),
-            pltpu.VMEM(wide, BF16),
-            pltpu.VMEM(wide, BF16),
-            pltpu.VMEM(wide, BF16),
-            pltpu.VMEM(wide, BF16),
-            pltpu.VMEM((C, SITES), F32),
-            pltpu.VMEM((C, SITES), F32),
-            pltpu.VMEM(wide, F32),
-            pltpu.VMEM(wide, F32),
+            pltpu.VMEM((192, SITES), BF16),
+            pltpu.VMEM(pair, BF16),
+            pltpu.VMEM(pair, BF16),
+            pltpu.VMEM(pair, BF16),
+            pltpu.VMEM((2, C, SITES), F32),
+            pltpu.VMEM((2, C, SITES), F32),
+            pltpu.VMEM(pair, F32),
+            pltpu.VMEM(pair, F32),
             pltpu.VMEM((2 * C, SITES), BF16),
         ],
         name="states",
@@ -324,12 +335,9 @@
     parts = lax.all_to_all(payload.reshape(32, CHUNK, LY), ("z", "x"), 0, 0, tiled=True)
     own_sum = jnp.sum(parts, axis=0)
     turned = lax.ppermute(own_sum, ("yh", "z", "x", "yl", "core"), turn_pairs())
-    other = lax.ppermute(own_sum, ("yh", "yl"), [(y, 7 - y) for y in range(8)])
     row = lax.broadcasted_iota(jnp.int32, (CHUNK, LY), 0)
-    own_sum, row, column = lax.optimization_barrier((own_sum, row, lax.broadcasted_iota(jnp.int32, (CHUNK, LY), 1)))
-    is_right = column >= C
-    small = jnp.where(is_right & (row == 3), own_sum, jnp.where(is_right & (row == 4), other, own_sum + other))
-    mixed = jnp.where(row < HEAD, small, turned)
+    own_sum, row = lax.optimization_barrier((own_sum, row))
+    mixed = jnp.where(row < HEAD, own_sum, turned)
     gathered = lax.all_to_all(
         jnp.broadcast_to(mixed, (8, CHUNK, LY)), ("yl", "core"), 0, 0, tiled=True
     )

time: 70.2 us -> 68.6 us (0.977)
  starting transfers between devices: 14.2 us -> 12.1 us
  Pallas kernels: 5.25 us -> 6.72 us
    ppermute x1 -> x0, starting transfers between devices: 2.18 us -> none  [local(): other = lax.ppermute(own_sum, ('yh', 'yl'), [(y, 7 - y) for y in range(8)])]
    ppermute x1 -> x0, waiting for transfers between devices: 1.51 us -> none  [local(): other = lax.ppermute(own_sum, ('yh', 'yl'), [(y, 7 - y) for y in range(8)])]
    ppermute x1, waiting for transfers between devices: 3.8 us -> 5.17 us  [local(): turned = lax.ppermute(own_sum, ('yh', 'z', 'x', 'yl', 'core'), turn_pairs())]
    pallas_call x1, Pallas kernels: 2.54 us -> 3.69 us  [local(): pl.pallas_call(states_kernel, out_shape=pltpu.VMEM((32 * CHUNK, LY), F32)...]
  transfers between devices with their start and end apart: 3 -> 2, of which waited for: 3 -> 2; matrix products, arithmetic and copies ran while one was open for 0% -> 0% of each run, Pallas kernels for 3% -> 3%
where the time goes in v7:
time: 68.6 us; the launch traced here: 68.3 us
  blocking collectives  37.7 us (55%)
  starting transfers between devices  12.1 us (18%)
  waiting for transfers between devices  9.91 us (14%)
  Pallas kernels  6.72 us (10%)
  local copies, waits for them, and re-layouts  1.27 us (2%)
    all_to_all x1, blocking collectives, local(): lax.all_to_all(payload.reshape(32, CHUNK, LY), ('z', 'x'), 0, 0, tiled=True)  24.9 us
    all_to_all x1, blocking collectives, local(): lax.all_to_all(jnp.broadcast_to(mixed, (8, CHUNK, LY)), ('yl', 'core'), 0...  12.8 us
    all_to_all x1, starting transfers between devices, local(): lax.all_to_all(own, ('yh', 'yl', 'core'), 0, 0, tiled=True)  10.1 us
    ppermute x1, waiting for transfers between devices, local(): turned = lax.ppermute(own_sum, ('yh', 'z', 'x', 'yl', 'core'), turn_pairs())  5.17 us
    all_to_all x1, waiting for transfers between devices, local(): lax.all_to_all(own, ('yh', 'yl', 'core'), 0, 0, tiled=True)  4.74 us
    pallas_call x1, Pallas kernels, local(): pl.pallas_call(states_kernel, out_shape=pltpu.VMEM((32 * CHUNK, LY), F32)...  3.69 us
    pallas_call x1, Pallas kernels, local(): pl.pallas_call(weights_kernel, out_shape=(pltpu.VMEM((2, 2, 192, 192), BF...  2.24 us
    ppermute x1, starting transfers between devices, local(): turned = lax.ppermute(own_sum, ('yh', 'z', 'x', 'yl', 'core'), turn_pairs())  1.92 us
  transfers between devices with their start and end apart: 2, of which 2 were waited for; matrix products, arithmetic and copies ran while one was open for 0% of the time, Pallas kernels for 3%

profile of v7, /device:TPU:1, one launch (start us, length us, event | category | flops | bytes accessed | tf_op | source)
XLA Modules:
  0.0 68.3 jit_solution(2356175713887866860)
XLA Ops:
  0.6 1.3 %broadcast_in_dim.11 = s32[16,1,128]{2,1,0:T(1,128)} broadcast(s32[128]{0:T(128)} %bitcast.8), dimensions={2} | broadcast | bytes 8704 | tf_op jit(solution)/shard_map/broadcast_in_dim | solution.py:296
  1.9 10.1 %all-to-all-start = ((s32[16,1,128]{2,1,0:T(1,128)}), s32[16,1,128]{2,1,0:T(1,128)S(1)}, u32[]{:S(2)}, u32[]{:S(2)}) async-start(s32[16,1,128]{2,1,0:T(1,128)} %broadcast_in_dim.11), calls=%async_computation | async-start | bytes 16384 | tf_op jit(solution)/shard_map/all_to_all | solution.py:297
  12.0 2.2 %weights.1 = (bf16[2,2,192,192]{3,2,1,0:T(8,128)(2,1)S(1)}, bf16[2,2,192,192]{3,2,1,0:T(8,128)(2,1)S(1)}, bf16[64,24]{1,0:T(8,128)(2,1)S(1)}, f32[2,3,64,128]{3,2,1,0:T(8,128)S(1)}) custom-call(bf16[9,64]{1,0:T(8,128)(2,1)} %bitcast.7, bf16[16,1,2,64,576]{4,3,2,1,0:T(8,128)(2,1)} %weight_hbm.1, bf16[16,64]{1,0:T(8,128)(2,1)} %readout_ref.1, f32[16,64]{1,0:T(8,128)} %cot_ref.1), custom_call_target="tpu_custom_call" | custom-call | tf_op jit(solution)/shard_map/weights/pallas_call | solution.py:300
  14.3 4.7 %all-to-all-done = s32[16,1,128]{2,1,0:T(1,128)S(1)} async-done(((s32[16,1,128]{2,1,0:T(1,128)}), s32[16,1,128]{2,1,0:T(1,128)S(1)}, u32[]{:S(2)}, u32[]{:S(2)}) %all-to-all-start) | async-done | bytes 8224 | tf_op jit(solution)/shard_map/all_to_all | solution.py:297
  19.0 3.7 %states.1 = f32[768,128]{1,0:T(8,128)S(1)} custom-call(s32[16,128]{1,0:T(8,128)S(1)} %bitcast.6, bf16[2,2,192,192]{3,2,1,0:T(8,128)(2,1)S(1)} %get-tuple-element.12.wf_ref, bf16[2,2,192,192]{3,2,1,0:T(8,128)(2,1)S(1)} %get-tuple-element.13.wt_ref, bf16[64,24]{1,0:T(8,128)(2,1)S(1)} %get-tuple-element.14.taps_ref, ...), custom_call_target="tpu_custom_call" | custom-call | tf_op jit(solution)/shard_map/states/pallas_call | solution.py:314
  22.7 24.9 %all_to_all.15 = f32[32,24,128]{2,1,0:T(8,128)S(1)} all-to-all(f32[32,24,128]{2,1,0:T(8,128)S(1)} %bitcast.5), channel_id=1, replica_groups=mesh['yh'=2,'z'=8,'x'=4,'yl'=4,'core'=2] {'z','x'}, dimensions={0} | all-to-all | bytes 786432 | tf_op jit(solution)/shard_map/all_to_all | solution.py:335
  47.7 1.9 %collective-permute-start = (f32[24,128]{1,0:T(8,128)S(1)}, f32[24,128]{1,0:T(8,128)S(1)}, u32[]{:S(2)}, u32[]{:S(2)}) collective-permute-start(f32[24,128]{1,0:T(8,128)S(1)} %reduce_sum.9), channel_id=1, source_target_pairs={{0,7},{1,231},{2,39},{3,199},{4,71},{5,167},{6,103},{7,135},{8,15}... | collective-permute-start | bytes 36872 | tf_op jit(solution)/shard_map/ppermute | solution.py:337
  49.6 5.2 %collective-permute-done = f32[24,128]{1,0:T(8,128)S(1)} collective-permute-done((f32[24,128]{1,0:T(8,128)S(1)}, f32[24,128]{1,0:T(8,128)S(1)}, u32[]{:S(2)}, u32[]{:S(2)}) %collective-permute-start) | collective-permute-done | bytes 12320 | tf_op jit(solution)/shard_map/ppermute | solution.py:337
  54.8 12.8 %all_to_all.16.all_ref = f32[8,24,128]{2,1,0:T(8,128)S(1)} all-to-all(f32[8,24,128]{2,1,0:T(8,128)S(1)} %broadcast_in_dim.12), channel_id=1, replica_groups=mesh['yh'=2,'z'=8,'x'=4,'yl'=4,'core'=2] {'yl','core'}, dimensions={0} | all-to-all | bytes 196608 | tf_op jit(solution)/shard_map/all_to_all | solution.py:341
  67.5 0.8 %outputs.1 = (f32[16,64]{1,0:T(8,128)}, f32[16,1,2,576]{3,2,1,0:T(2,128)}, f32[9,64]{1,0:T(8,128)}) custom-call(f32[8,24,128]{2,1,0:T(8,128)S(1)} %all_to_all.16.all_ref), custom_call_target="tpu_custom_call" | custom-call | tf_op jit(solution)/shard_map/outputs/pallas_call | solution.py:345
  (4 shorter events, 0.1 us)
Async XLA Ops:
  1.9 17.1 %all-to-all-start = ((s32[16,1,128]{2,1,0:T(1,128)}), s32[16,1,128]{2,1,0:T(1,128)S(1)}, u32[]{:S(2)}, u32[]{:S(2)}) async-start(s32[16,1,128]{2,1,0:T(1,128)} %broadcast_in_dim.11), calls=%async_computation | async-start | bytes 16384 | tf_op jit(solution)/shard_map/all_to_all | solution.py:297
  47.7 7.1 %collective-permute-start = (f32[24,128]{1,0:T(8,128)S(1)}, f32[24,128]{1,0:T(8,128)S(1)}, u32[]{:S(2)}, u32[]{:S(2)}) collective-permute-start(f32[24,128]{1,0:T(8,128)S(1)} %reduce_sum.9), channel_id=1, source_target_pairs={{0,7},{1,231},{2,39},{3,199},{4,71},{5,167},{6,103},{7,135},{8,15}... | collective-permute-start | bytes 36872 | tf_op jit(solution)/shard_map/ppermute | solution.py:337
